TPU v7x, 256 devices: a whole 4x4x8 slice. The times are simulated.
256 devices in a mesh: hid: 4 (over x_lo, core), tok: 64 (over x_hi, y, z).
Axes of the slice: x: 4 (x_hi: 2, x_lo: 2; x = x_hi * 2 + x_lo), y: 4, z: 8, core: 2. Of those that a mesh axis runs over, the one named last changes fastest.
Arguments:
- val_inputs: bfloat16 [256, 4096], P(None, 'tok'), may hold values from -6 to 6
- val_out_grad: bfloat16 [256, 4096], P(None, 'tok'), may hold values from -6 to 6
- w_gate: bfloat16 [4096, 14336], P('tok', 'hid'), may hold values from -0.09375 to 0.09375
- w_up: bfloat16 [4096, 14336], P('tok', 'hid'), may hold values from -0.09375 to 0.09375
- w_down: bfloat16 [14336, 4096], P('hid', 'tok'), may hold values from -0.046875 to 0.046875
- val_attn_inputs: bfloat16 [256, 4096], P('hid', 'tok'), may hold values from -6 to 6
- train_inputs: bfloat16 [163840, 4096], P(('hid', 'tok')), may hold values from -6 to 6
- train_grads: bfloat16 [163840, 4096], P(('hid', 'tok')), may hold values from -6 to 6
Outputs:
- influence: float32 [163840], P(('hid', 'tok'))
- val_grad: bfloat16 [256, 4096], P('hid', 'tok')
All inputs are finite; a program needn't handle non-finite values.
Results may differ from a plain program's by a relative error of at most 0.0036.
Values may be sent and summed in bfloat16 or wider, within the bound.
No kernel may reach another device: no remote copies, remote signals or barrier semaphores. Data moves between devices by JAX's collectives and lax.ppermute only.
A program may use at most 128 MiB of HBM per device.

v0:
```python
import math

import jax
import jax.numpy as jnp
from jax import lax
from jax.sharding import PartitionSpec as P


def dot_rows(left, right):
    return lax.dot_general(
        left, right, (((1,), (1,)), ((), ())), preferred_element_type=jnp.float32
    )


def act_grads(gate_pre, up_pre, hid_grad):
    logistic = jax.nn.sigmoid(gate_pre)
    grad_gate = (hid_grad * up_pre * logistic * (1.0 + gate_pre * (1.0 - logistic))).astype(
        jnp.bfloat16
    )
    grad_up = (hid_grad * gate_pre * logistic).astype(jnp.bfloat16)
    return (grad_gate, grad_up)


def pair_terms(train_in, train_gr, val_in, val_gr):
    in_gram = dot_rows(train_in, val_in)
    grad_gram = dot_rows(train_gr, val_gr)
    return jnp.sum(in_gram * grad_gram, axis=1)


def local(
    val_inputs, val_out_grad, w_gate, w_up, w_down, val_attn_inputs, train_inputs, train_grads
):
    hid_units = w_gate.shape[1]
    val_count = val_out_grad.shape[0]
    gate_pre = jnp.dot(val_inputs, w_gate, preferred_element_type=jnp.float32)
    up_pre = jnp.dot(val_inputs, w_up, preferred_element_type=jnp.float32)
    hid_grad = dot_rows(val_out_grad, w_down)
    sums = lax.psum_scatter(
        jnp.concatenate([gate_pre, up_pre, hid_grad], axis=1),
        "tok",
        scatter_dimension=0,
        tiled=True,
    )
    grad_gate, grad_up = act_grads(
        sums[:, :hid_units], sums[:, hid_units : 2 * hid_units], sums[:, 2 * hid_units :]
    )
    stacked = jnp.concatenate([grad_gate, grad_up], axis=1)
    piece = lax.all_gather(stacked, "tok", axis=0, tiled=True)
    dx_part = dot_rows(piece[:, :hid_units], w_gate) + dot_rows(piece[:, hid_units:], w_up)
    quarter = val_count // lax.axis_size("hid")
    first_row = lax.axis_index("hid") * quarter
    dx_rows = lax.psum_scatter(dx_part, "hid", scatter_dimension=0, tiled=True)
    own_rows = lax.dynamic_slice_in_dim(val_out_grad, first_row, quarter, 0)
    val_grad = (own_rows.astype(jnp.float32) + dx_rows).astype(jnp.bfloat16)
    attn_full, grad_full = (
        lax.all_gather(val_attn_inputs, "tok", axis=1, tiled=True),
        lax.all_gather(val_grad, "tok", axis=1, tiled=True),
    )
    total = pair_terms(
        train_inputs,
        train_grads,
        lax.all_gather(attn_full, "hid", axis=0, tiled=True),
        lax.all_gather(grad_full, "hid", axis=0, tiled=True),
    )
    influence = total / (train_inputs.shape[1] * math.sqrt(val_count))
    return (influence, val_grad)


def solution(mesh):
    placed = (
        P(None, "tok"),
        P(None, "tok"),
        P("tok", "hid"),
        P("tok", "hid"),
        P("hid", "tok"),
        P("hid", "tok"),
        P(("hid", "tok"), None),
        P(("hid", "tok"), None),
    )
    return jax.shard_map(
        local,
        mesh=mesh,
        in_specs=placed,
        out_specs=(P(("hid", "tok")), P("hid", "tok")),
        check_vma=False,
    )
```

profile of v0, /device:TPU:1, one launch (start us, length us, event | category | flops | bytes accessed | tf_op | source)
XLA Modules:
  0.0 1299.6 jit_solution(1939003087148605138)
XLA Ops:
  7.2 0.0 copy-start
  7.2 0.0 copy-start.3
  7.2 0.0 copy-start.1
  7.2 0.0 copy-start.4
  7.2 0.0 all-reduce.3.cloned.1.call-start
  7.3 1.8 fusion.13
  9.0 0.0 copy-done
  9.0 0.0 copy-done.3
  9.0 0.7 fusion.14
  9.7 0.0 copy-done.1
  9.7 0.7 fusion.15
  10.4 4.4 pad_maximum_fusion
  14.8 0.0 all-reduce.3.cloned.1.call-update
  14.8 0.0 all-gather.9.cloned.1.call-start
  14.8 0.6 copy-done.7
  15.4 0.6 dynamic-slice
  16.7 697.3 %all-reduce.3.cloned.1.call-done = f32[256,10752]{1,0:T(8,128)} async-done(((f32[256,10752]{1,0:T(8,128)}), f32[256,10752]{1,0:T(8,128)}) %all-reduce.3.cloned.1.call-update) | async-done | bytes 11010064
  713.9 1.1 fusion.11
  715.1 0.6 maximum_bitcast_fusion
  715.7 0.0 all-gather.9.cloned.1.call-update
  715.7 0.0 reduce-scatter.2.cloned.1.call-start
  715.8 0.0 copy-done.6
  715.8 0.1 copy.14
  715.9 0.0 copy-start.2
  715.9 162.7 %all-gather.9.cloned.1.call-done = bf16[64,4,7168]{2,1,0:T(4,128)(2,1)} async-done(((bf16[1,4,7168]{2,1,0:T(4,128)(2,1)}), bf16[64,4,7168]{2,1,0:T(4,128)(2,1)}) %all-gather.9.cloned.1.call-update) | async-done | bytes 3670032 | tf_op jit(solution)/shard_map/all_gather | solution.py:48
  878.6 6.7 reshape.5
  885.3 2.1 fusion
  887.4 2.8 fusion.6
  890.2 0.0 reduce-scatter.2.cloned.1.call-update
  890.2 0.0 all-gather.5.cloned.1.call-start
  890.3 155.9 %all_gather.15 = bf16[64,4096]{0,1:T(8,128)(2,1)S(1)} all-gather(bf16[64,64]{0,1:T(8,128)(2,1)S(1)} %copy.14), channel_id=1, replica_groups=mesh['hid'=4,'tok'=64] {'tok'}, dimensions={1}, use_global_device_ids=true | all-gather | bytes 532480 | tf_op jit(solution)/shard_map/all_gather | solution.py:56
  1046.2 1.1 copy.15
  1047.3 0.0 all-gather.5.cloned.1.call-update
  1047.3 0.0 all-gather.7.cloned.1.call-start
  1047.4 0.1 constant_dynamic-slice_fusion
  1047.5 0.1 copy.19
  1047.6 0.0 reduce-scatter.2.cloned.1.call-done
  1047.6 0.8 add_convert_fusion
  1048.4 0.1 copy.17
  1048.4 153.2 %all_gather.18 = bf16[64,4096]{0,1:T(8,128)(2,1)S(1)} all-gather(bf16[64,64]{0,1:T(8,128)(2,1)S(1)} %copy.17), channel_id=1, replica_groups=mesh['hid'=4,'tok'=64] {'tok'}, dimensions={1}, use_global_device_ids=true | all-gather | bytes 532480 | tf_op jit(solution)/shard_map/all_gather | solution.py:57
  1201.7 1.1 copy.18
  1202.8 0.0 all-gather.7.cloned.1.call-update
  1202.8 0.0 all-gather.5.cloned.1.call-done
  1202.9 5.0 fusion.12
  1207.9 0.0 copy-done.5
  1207.9 79.7 %all-gather.7.cloned.1.call-done = bf16[256,4096]{1,0:T(8,128)(2,1)} async-done(((bf16[64,4096]{1,0:T(8,128)(2,1)}), bf16[256,4096]{1,0:T(8,128)(2,1)}) %all-gather.7.cloned.1.call-update) | async-done | bytes 2097168 | tf_op jit(solution)/shard_map/all_gather | solution.py:63
  1287.5 5.0 fusion.5
  1292.5 0.6 broadcast_multiply_fusion
  (5 shorter events, 0.0 us)
Async XLA Ops:
  7.2 1.9 copy-start
  7.2 1.8 copy-start.3
  7.2 2.5 copy-start.1
  7.2 2.5 copy-start.4
  7.2 706.7 %all-reduce.3.cloned.1.call-start = ((), (), s32[]{:S(2)}) async-start(), calls=%async_computation.5 | async-start | bytes 22020096
  14.8 0.7 copy-start.7
  14.8 701.0 %copy-start.6 = (bf16[64,64]{1,0:T(8,128)(2,1)S(1)}, bf16[64,64]{1,0:T(8,128)(2,1)}, u32[]{:S(2)}) copy-start(bf16[64,64]{1,0:T(8,128)(2,1)} %param.13) | copy-start | bytes 24580
  14.8 863.8 %all-gather.9.cloned.1.call-start = ((), (), s32[]{:S(2)}) async-start(), calls=%async_computation.4 | async-start | bytes 3727360 | tf_op jit(solution)/shard_map/all_gather | solution.py:48
  715.7 331.8 %reduce-scatter.2.cloned.1.call-start = ((), (), s32[]{:S(2)}) async-start(), calls=%async_computation.2 | async-start | bytes 163840 | tf_op jit(solution)/shard_map/reduce_scatter | solution.py:52
  715.9 171.5 %copy-start.2 = (bf16[64,3584]{1,0:T(8,128)(2,1)S(1)}, bf16[64,3584]{1,0:T(8,128)(2,1)}, u32[]{:S(2)}) copy-start(bf16[64,3584]{1,0:T(8,128)(2,1)} %param.10) | copy-start | bytes 1376260
  890.2 312.6 %all-gather.5.cloned.1.call-start = ((), (), s32[]{:S(2)}) async-start(), calls=%async_computation.1 | async-start | bytes 2621440 | tf_op jit(solution)/shard_map/all_gather | solution.py:62
  1047.3 240.2 %all-gather.7.cloned.1.call-start = ((), (), s32[]{:S(2)}) async-start(), calls=%async_computation.3 | async-start | bytes 2621440 | tf_op jit(solution)/shard_map/all_gather | solution.py:63
  1048.4 159.5 %copy-start.5 = (bf16[64,64]{1,0:T(8,128)(2,1)}, bf16[64,64]{1,0:T(8,128)(2,1)S(1)}, u32[]{:S(2)}) copy-start(bf16[64,64]{1,0:T(8,128)(2,1)S(1)} %add_convert_fusion) | copy-start | bytes 24580
Sparse Core Ops, SparseCore 0:
  14.9 698.9 all-reduce.2
  717.4 161.1 all-gather.8
  890.4 20.3 reduce-scatter.1
  1047.4 56.4 all-gather.4
  1203.0 84.5 all-gather.6
where the time goes:
time: 1300 us
  waiting for transfers between devices  940 us (72%)
  blocking collectives  309 us (24%)
  matrix products  17.9 us (1%)
  between operations  14.6 us (1%)
    unnamed x6, waiting for transfers between devices  697 us
    all_gather x1, waiting for transfers between devices, local(): piece = lax.all_gather(stacked, 'tok', axis=0, tiled=True)  163 us
    all_gather x1, blocking collectives, local(): lax.all_gather(val_attn_inputs, 'tok', axis=1, tiled=True)  156 us
    all_gather x1, blocking collectives, local(): lax.all_gather(val_grad, 'tok', axis=1, tiled=True)  153 us
    all_gather x1, waiting for transfers between devices, local(): lax.all_gather(grad_full, 'hid', axis=0, tiled=True)  79.7 us
  transfers between devices with their start and end apart: 5, of which 3 were waited for; matrix products, arithmetic and copies ran while one was open for 1% of the time, Pallas kernels for 0%

commit v1 on v0

v1 whole, which is shorter than its diff:
```python
import math

import jax
import jax.numpy as jnp
from jax import lax
from jax.sharding import Mesh
from jax.sharding import PartitionSpec as P

PLANE = ("xh", "y")
CHIPS = ("xl", "xh", "y")
HIDPLANE = ("xl", "c", "xh", "y")
BF16 = jnp.bfloat16
F32 = jnp.float32


def trade(value, axes):
    return lax.all_to_all(value, axes, 0, 0, tiled=True)


def share(value, axes, count):
    return trade(jnp.broadcast_to(value[None], (count,) + value.shape), axes)


def dot_first(left, right):
    return lax.dot_general(left, right, (((0,), (0,)), ((), ())), preferred_element_type=F32)


def dot_last(left, right):
    return lax.dot_general(left, right, (((1,), (1,)), ((), ())), preferred_element_type=F32)


def act_grads(gate_pre, up_pre, hid_grad):
    logistic = jax.nn.sigmoid(gate_pre)
    grad_gate = (hid_grad * up_pre * logistic * (1.0 + gate_pre * (1.0 - logistic))).astype(BF16)
    grad_up = (hid_grad * gate_pre * logistic).astype(BF16)
    return jnp.concatenate([grad_gate, grad_up], axis=1)


def local(
    val_inputs, val_out_grad, w_gate, w_up, w_down, val_attn_inputs, train_inputs, train_grads
):
    feats, units = w_gate.shape
    vals = val_inputs.shape[0]
    n_plane = lax.axis_size(PLANE)
    n_z = lax.axis_size("z")
    n_chips = lax.axis_size(CHIPS)
    n_hidplane = lax.axis_size(HIDPLANE)
    own = units // n_plane
    wide = feats * n_plane

    def spread(weight):
        return weight.reshape(feats, n_plane, own)

    def same(value):
        return jnp.broadcast_to(value[:, None], (feats, n_plane, vals))

    sent = jnp.concatenate(
        [
            spread(w_gate),
            spread(w_up),
            spread(w_down.T),
            same(val_inputs.T),
            same(val_out_grad.T),
        ],
        axis=2,
    ).transpose(1, 0, 2)
    got = trade(sent, PLANE).reshape(wide, 3 * own + 2 * vals)
    gate_w, up_w, down_w = got[:, :own], got[:, own : 2 * own], got[:, 2 * own : 3 * own]
    inputs_t, out_grad_t = got[:, 3 * own : 3 * own + vals], got[:, 3 * own + vals :]
    partial = jnp.concatenate(
        [dot_first(inputs_t, got[:, : 2 * own]), dot_first(out_grad_t, down_w)], axis=1
    ).astype(BF16)
    rows_z = vals // n_z
    pre = jnp.sum(trade(partial.reshape(n_z, rows_z, 3 * own), "z").astype(F32), axis=0)
    grads = act_grads(pre[:, :own], pre[:, own : 2 * own], pre[:, 2 * own :])
    attn_rows = val_attn_inputs.shape[0]
    attn_wide = attn_rows * feats // rows_z
    back = share(
        jnp.concatenate([grads, val_attn_inputs.reshape(rows_z, attn_wide)], axis=1), "z", n_z
    )
    grads = back[:, :, : 2 * own].reshape(vals, 2 * own)
    attn = back[:, :, 2 * own :].reshape(n_z, attn_rows, feats)
    part = dot_last(grads[:, :own], gate_w) + dot_last(grads[:, own:], up_w)
    chunk = vals // n_hidplane
    dx = jnp.sum(trade(part.reshape(n_hidplane, chunk, wide), HIDPLANE), axis=0)
    row = lax.axis_index(HIDPLANE) * chunk
    mine = lax.dynamic_slice_in_dim(out_grad_t, row, chunk, 1).T
    val_grad = (mine.astype(F32) + dx).astype(BF16)
    width = train_inputs.shape[1]
    val_z = share(val_grad, "z", n_z).reshape(n_z, chunk, n_plane, feats)
    val_z = val_z.transpose(1, 2, 0, 3).reshape(chunk, width)
    attn_z = attn.transpose(1, 0, 2).reshape(attn_rows // chunk, chunk, n_z * feats)
    attn_z = attn_z.transpose(1, 0, 2).reshape(chunk, attn_rows * feats * n_z // chunk)
    both = share(jnp.concatenate([val_z, attn_z], axis=1), CHIPS, n_chips)
    swap = [(0, 1), (1, 0)]
    other = lax.ppermute(both, "c", swap)
    xl_size = n_chips // n_plane

    def rows_of(block):
        val_rows = block[:, :, :width].reshape(n_chips * chunk, width)
        att = block[:, :, width:].reshape(xl_size, n_plane, chunk, attn_rows // chunk, n_z * feats)
        att = att.transpose(0, 3, 2, 1, 4).reshape(xl_size * attn_rows, width)
        return val_rows, att

    val_a, att_a = rows_of(both)
    val_b, att_b = rows_of(other)
    val_all = jnp.concatenate([val_a, val_b], axis=0)
    att_all = jnp.concatenate([att_a, att_b], axis=0)
    total = jnp.sum(dot_last(train_inputs, att_all) * dot_last(train_grads, val_all), axis=1)
    influence = total / (width * math.sqrt(vals))
    block = lax.dynamic_slice(
        val_a,
        (lax.axis_index("xl") * attn_rows, lax.axis_index(("xh", "y", "z")) * feats),
        (attn_rows, feats),
    )
    return (influence, block)


def solution(mesh):
    fine = Mesh(mesh.devices.reshape(2, 2, 2, 4, 8), ("xl", "c", "xh", "y", "z"))
    tok = ("xh", "y", "z")
    hid = ("xl", "c")
    placed = (
        P(None, tok),
        P(None, tok),
        P(tok, hid),
        P(tok, hid),
        P(hid, tok),
        P(hid, tok),
        P(hid + tok, None),
        P(hid + tok, None),
    )
    return jax.shard_map(
        local,
        mesh=fine,
        in_specs=placed,
        out_specs=(P(hid + tok), P(hid, tok)),
        check_vma=False,
    )
```

time: 1300 us -> 167 us (0.13)
  waiting for transfers between devices: 940 us -> 38.9 us
  blocking collectives: 309 us -> 79.5 us
  starting transfers between devices: 0.21 us -> 23.5 us
  between operations: 14.6 us -> 1.04 us
    unnamed x6 -> x0, waiting for transfers between devices: 697 us -> none
    all_gather x2 -> x0, blocking collectives: 309 us -> none  [the longest x1 156 us: local(): lax.all_gather(val_attn_inputs, 'tok', axis=1, tiled=True)]
    all_gather x3 -> x0, waiting for transfers between devices: 242 us -> none  [the longest x1 163 us: local(): piece = lax.all_gather(stacked, 'tok', axis=0, tiled=True)]
    all_to_all x0 -> x3, blocking collectives: none -> 79.5 us  [trade(): return lax.all_to_all(value, axes, 0, 0, tiled=True)]
    all_to_all x0 -> x3, waiting for transfers between devices: none -> 36.8 us  [trade(): return lax.all_to_all(value, axes, 0, 0, tiled=True)]
    all_to_all x0 -> x3, starting transfers between devices: none -> 20.1 us  [trade(): return lax.all_to_all(value, axes, 0, 0, tiled=True)]
  transfers between devices with their start and end apart: 5 -> 4, of which waited for: 3 -> 4; matrix products, arithmetic and copies ran while one was open for 1% -> 2% of each run, Pallas kernels for 0% -> 0%
where the time goes in v1:
time: 167 us; the launch traced here: 166 us
  blocking collectives  79.5 us (48%)
  waiting for transfers between devices  38.9 us (23%)
  starting transfers between devices  23.5 us (14%)
  local copies, waits for them, and re-layouts  15.2 us (9%)
  matrix products  6.35 us (4%)
  other arithmetic  1.87 us (1%)
    all_to_all x3, blocking collectives, trade(): return lax.all_to_all(value, axes, 0, 0, tiled=True)  79.5 us
    all_to_all x3, waiting for transfers between devices, trade(): return lax.all_to_all(value, axes, 0, 0, tiled=True)  36.8 us
    all_to_all x3, starting transfers between devices, trade(): return lax.all_to_all(value, axes, 0, 0, tiled=True)  20.1 us
    dot_general x4, matrix products, dot_last(): lax.dot_general(left, right, (((1,), (1,)), ((), ())), preferred_element_...  5.37 us
    reshape x6, local copies, waits for them, and re-layouts, spread(): return weight.reshape(feats, n_plane, own)  3.41 us
    ppermute x1, starting transfers between devices, local(): other = lax.ppermute(both, 'c', swap)  3.35 us
  transfers between devices with their start and end apart: 4, of which 4 were waited for; matrix products, arithmetic and copies ran while one was open for 2% of the time, Pallas kernels for 0%

profile of v1, /device:TPU:1, one launch (start us, length us, event | category | flops | bytes accessed | tf_op | source)
XLA Modules:
  0.0 166.3 jit_solution(14852551562320998619)
XLA Ops:
  0.7 1.7 %reshape.68 = bf16[64,8,448]{2,1,0:T(8,128)(2,1)S(1)} reshape(bf16[64,3584]{1,0:T(8,128)(2,1)} %param.10) | data formatting | bytes 917504 | tf_op jit(solution)/shard_map/reshape | solution.py:52
  2.4 0.2 copy.26
  2.6 0.6 reshape.69
  3.2 0.2 copy.27
  3.4 0.6 reshape.70
  4.0 0.2 copy.28
  4.2 0.7 broadcast_in_dim.10
  4.9 0.7 broadcast_in_dim.11
  5.6 2.6 %concatenate.24 = bf16[64,8,1856]{2,0,1:T(8,128)(2,1)S(1)} concatenate(bf16[64,8,448]{2,0,1:T(8,128)(2,1)S(1)} %copy.26, bf16[64,8,448]{2,0,1:T(8,128)(2,1)S(1)} %copy.27, bf16[64,8,448]{2,0,1:T(8,128)(2,1)S(1)} %copy.28, bf16[64,8,256]{2,0,1:T(8,128)(2,1)} %broadcast_in_dim.10, bf16[64,8,256]{2,0,1:T(8,128)(2,1)} %broadcast_in_dim.11), dimensions={2} | concatenate | bytes 3801088 | tf_op jit(solution)/shard_map/concatenate | solution.py:57
  8.2 33.1 %all_to_all.30 = bf16[8,64,1856]{2,1,0:T(8,128)(2,1)S(1)} all-to-all(bf16[8,64,1856]{2,1,0:T(8,128)(2,1)S(1)} %bitcast.49), channel_id=1, replica_groups=mesh['xl'=2,'c'=2,'xh'=2,'y'=4,'z'=8] {'xh','y'}, dimensions={0} | all-to-all | bytes 3801088 | tf_op jit(solution)/shard_map/all_to_all | solution.py:17
  41.3 0.4 convolution_convert_fusion.1
  41.7 0.9 copy-done
  42.6 0.5 convolution_convert_fusion
  43.2 0.1 copy.30
  43.3 0.9 pad_maximum_fusion
  44.2 8.2 %all-to-all-start.1 = ((bf16[8,32,1344]{2,1,0:T(8,128)(2,1)}), bf16[8,32,1344]{2,1,0:T(8,128)(2,1)S(1)}, u32[]{:S(2)}, u32[]{:S(2)}) async-start(bf16[8,32,1344]{2,1,0:T(8,128)(2,1)} %pad_maximum_fusion), calls=%async_computation.1 | async-start | bytes 1441792 | tf_op jit(solution)/shard_map/all_to_all | solution.py:17
  52.5 19.7 %all-to-all-done.1 = bf16[8,32,1344]{2,1,0:T(8,128)(2,1)S(1)} async-done(((bf16[8,32,1344]{2,1,0:T(8,128)(2,1)}), bf16[8,32,1344]{2,1,0:T(8,128)(2,1)S(1)}, u32[]{:S(2)}, u32[]{:S(2)}) %all-to-all-start.1) | async-done | bytes 688160 | tf_op jit(solution)/shard_map/all_to_all | solution.py:17
  72.3 0.1 convert_reduce_fusion
  72.4 0.1 fusion.25
  72.6 16.7 %all_to_all.31 = bf16[8,32,1024]{2,1,0:T(8,128)(2,1)S(1)} all-to-all(bf16[8,32,1024]{2,1,0:T(8,128)(2,1)S(1)} %broadcast_in_dim.12), channel_id=1, replica_groups=mesh['xl'=2,'c'=2,'xh'=2,'y'=4,'z'=8] {'z'}, dimensions={0} | all-to-all | bytes 1048576 | tf_op jit(solution)/shard_map/all_to_all | solution.py:17
  89.4 0.3 fusion.17
  89.7 1.2 fusion.11
  91.0 8.6 %all-to-all-start.3 = ((f32[32,8,512]{2,1,0:T(8,128)}), f32[32,8,512]{2,1,0:T(8,128)S(1)}, u32[]{:S(2)}, u32[]{:S(2)}) async-start(f32[32,8,512]{2,1,0:T(8,128)} %fusion.11), calls=%async_computation.3 | async-start | bytes 1048576 | tf_op jit(solution)/shard_map/all_to_all | solution.py:17
  99.6 0.1 slice.68
  99.7 0.1 constant_dynamic-slice_fusion
  99.9 10.2 %all-to-all-done.3 = f32[32,8,512]{2,1,0:T(8,128)S(1)} async-done(((f32[32,8,512]{2,1,0:T(8,128)}), f32[32,8,512]{2,1,0:T(8,128)S(1)}, u32[]{:S(2)}, u32[]{:S(2)}) %all-to-all-start.3) | async-done | bytes 524320 | tf_op jit(solution)/shard_map/all_to_all | solution.py:17
  110.2 0.6 broadcast_in_dim.13
  110.9 3.3 %all-to-all-start.4 = ((bf16[8,8,512]{2,1,0:T(8,128)(2,1)}), bf16[8,8,512]{2,1,0:T(8,128)(2,1)S(1)}, u32[]{:S(2)}, u32[]{:S(2)}) async-start(bf16[8,8,512]{2,1,0:T(8,128)(2,1)} %broadcast_in_dim.13), calls=%async_computation.4 | async-start | bytes 131072 | tf_op jit(solution)/shard_map/all_to_all | solution.py:17
  114.2 0.1 reshape.77
  114.4 0.1 reshape.78
  114.6 6.9 %all-to-all-done.4 = bf16[8,8,512]{2,1,0:T(8,128)(2,1)S(1)} async-done(((bf16[8,8,512]{2,1,0:T(8,128)(2,1)}), bf16[8,8,512]{2,1,0:T(8,128)(2,1)S(1)}, u32[]{:S(2)}, u32[]{:S(2)}) %all-to-all-start.4) | async-done | bytes 65568 | tf_op jit(solution)/shard_map/all_to_all | solution.py:17
  121.4 0.1 reshape.75
  121.7 0.2 reshape.76
  121.9 0.2 broadcast_in_dim.14
  122.1 29.6 %all_to_all.32 = bf16[16,8,8192]{2,1,0:T(8,128)(2,1)S(1)} all-to-all(bf16[16,8,8192]{2,1,0:T(8,128)(2,1)S(1)} %broadcast_in_dim.14), channel_id=1, replica_groups=mesh['xl'=2,'c'=2,'xh'=2,'y'=4,'z'=8] {'xl','xh','y'}, dimensions={0} | all-to-all | bytes 4194304 | tf_op jit(solution)/shard_map/all_to_all | solution.py:17
  151.7 3.4 %collective-permute-start = (bf16[16,8,8192]{2,1,0:T(8,128)(2,1)S(1)}, bf16[16,8,8192]{2,1,0:T(8,128)(2,1)}, u32[]{:S(2)}, u32[]{:S(2)}) collective-permute-start(bf16[16,8,8192]{2,1,0:T(8,128)(2,1)S(1)} %all_to_all.32), channel_id=1, source_target_pairs={{0,64},{64,0},{1,65},{65,1},{2,66},{66,2},{3,67},{67,3},{4,68},{68... | collective-permute-start | bytes 6291464 | tf_op jit(solution)/shard_map/ppermute | solution.py:96
  155.1 0.1 slice_bitcast_fusion.1
  155.2 0.6 copy.33
  155.8 0.4 copy.38
  156.2 0.7 dynamic_slice.7
  156.9 2.1 %collective-permute-done = bf16[16,8,8192]{2,1,0:T(8,128)(2,1)} collective-permute-done((bf16[16,8,8192]{2,1,0:T(8,128)(2,1)S(1)}, bf16[16,8,8192]{2,1,0:T(8,128)(2,1)}, u32[]{:S(2)}, u32[]{:S(2)}) %collective-permute-start) | collective-permute-done | bytes 2097184 | tf_op jit(solution)/shard_map/ppermute | solution.py:96
  159.0 1.7 %slice_bitcast_fusion = (bf16[128,4096]{1,0:T(8,128)(2,1)S(1)}, bf16[16,8,4096]{2,1,0:T(8,128)(2,1)S(1)}) fusion(bf16[16,8,8192]{2,1,0:T(8,128)(2,1)} %collective-permute-done), kind=kLoop, calls=%fused_computation.15 | loop fusion | bytes 4194304 | tf_op jit(solution)/shard_map/reshape | solution.py:100
  160.7 0.6 copy.34
  161.3 0.4 copy.40
  161.7 2.0 %fusion = f32[256,640]{1,0:T(8,128)S(1)} fusion(bf16[640,4096]{1,0:T(8,128)(2,1)S(1)} %bitcast.72, bf16[128,4096]{1,0:T(8,128)(2,1)S(1)} %bitcast.62, bf16[128,4096]{1,0:T(8,128)(2,1)S(1)} %bitcast.61), kind=kOutput, calls=%fused_computation | convolution fusion | flops 1346371584 | bytes 7995392 | tf_op jit(solution)/shard_map/dot_general | solution.py:29
  163.7 0.2 slice-done.3
  163.9 1.8 %fusion.12 = f32[640]{0:T(1024)S(1)} fusion(f32[256,640]{1,0:T(8,128)S(1)} %fusion, bf16[640,4096]{1,0:T(8,128)(2,1)S(1)} %bitcast.74, bf16[128,4096]{1,0:T(8,128)(2,1)S(1)} %get-tuple-element.4, bf16[128,4096]{1,0:T(8,128)(2,1)S(1)} %get-tuple-element.2), kind=kOutput, calls=%fused_computation.14 | convolution fusion | flops 1346698624 | bytes 7997952 | tf_op jit(solution)/shard_map/dot_general | solution.py:29
  165.7 0.6 broadcast_multiply_fusion
  (33 shorter events, 0.7 us)
Async XLA Ops:
  0.6 1.9 %copy-start.2 = (bf16[64,3584]{1,0:T(8,128)(2,1)S(1)}, bf16[64,3584]{1,0:T(8,128)(2,1)}, u32[]{:S(2)}) copy-start(bf16[64,3584]{1,0:T(8,128)(2,1)} %param.11) | copy-start | bytes 1376260
  0.6 2.7 %copy-start.3 = (bf16[3584,64]{0,1:T(8,128)(2,1)S(1)}, bf16[3584,64]{0,1:T(8,128)(2,1)}, u32[]{:S(2)}) copy-start(bf16[3584,64]{0,1:T(8,128)(2,1)} %param.12) | copy-start | bytes 1376260
  2.5 1.6 copy-start.4
  2.5 2.3 %copy-start.5 = (bf16[256,64]{0,1:T(8,128)(2,1)S(1)}, bf16[256,64]{0,1:T(8,128)(2,1)}, u32[]{:S(2)}) copy-start(bf16[256,64]{0,1:T(8,128)(2,1)} %param.9) | copy-start | bytes 98308
  41.3 1.3 copy-start
  43.2 9.3 %copy-start.6 = (bf16[64,64]{1,0:T(8,128)(2,1)S(1)}, bf16[64,64]{1,0:T(8,128)(2,1)}, u32[]{:S(2)}) copy-start(bf16[64,64]{1,0:T(8,128)(2,1)} %param.13) | copy-start | bytes 24580
  44.2 28.0 %all-to-all-start.1 = ((bf16[8,32,1344]{2,1,0:T(8,128)(2,1)}), bf16[8,32,1344]{2,1,0:T(8,128)(2,1)S(1)}, u32[]{:S(2)}, u32[]{:S(2)}) async-start(bf16[8,32,1344]{2,1,0:T(8,128)(2,1)} %pad_maximum_fusion), calls=%async_computation.1 | async-start | bytes 1441792 | tf_op jit(solution)/shard_map/all_to_all | solution.py:17
  52.4 37.0 %copy-start.1 = (bf16[8,64,1856]{2,1,0:T(8,128)(2,1)S(1)}, bf16[8,64,1856]{2,1,0:T(8,128)(2,1)}, u32[]{:S(2)}) copy-start(bf16[8,64,1856]{2,1,0:T(8,128)(2,1)} %copy-done) | copy-start | bytes 5701636
  91.0 19.2 %all-to-all-start.3 = ((f32[32,8,512]{2,1,0:T(8,128)}), f32[32,8,512]{2,1,0:T(8,128)S(1)}, u32[]{:S(2)}, u32[]{:S(2)}) async-start(f32[32,8,512]{2,1,0:T(8,128)} %fusion.11), calls=%async_computation.3 | async-start | bytes 1048576 | tf_op jit(solution)/shard_map/all_to_all | solution.py:17
  110.9 10.6 %all-to-all-start.4 = ((bf16[8,8,512]{2,1,0:T(8,128)(2,1)}), bf16[8,8,512]{2,1,0:T(8,128)(2,1)S(1)}, u32[]{:S(2)}, u32[]{:S(2)}) async-start(bf16[8,8,512]{2,1,0:T(8,128)(2,1)} %broadcast_in_dim.13), calls=%async_computation.4 | async-start | bytes 131072 | tf_op jit(solution)/shard_map/all_to_all | solution.py:17
  151.7 7.3 %collective-permute-start = (bf16[16,8,8192]{2,1,0:T(8,128)(2,1)S(1)}, bf16[16,8,8192]{2,1,0:T(8,128)(2,1)}, u32[]{:S(2)}, u32[]{:S(2)}) collective-permute-start(bf16[16,8,8192]{2,1,0:T(8,128)(2,1)S(1)} %all_to_all.32), channel_id=1, source_target_pairs={{0,64},{64,0},{1,65},{65,1},{2,66},{66,2},{3,67},{67,3},{4,68},{68... | collective-permute-start | bytes 6291464 | tf_op jit(solution)/shard_map/ppermute | solution.py:96
  155.8 5.9 %slice-start = ((s8[5242880]{0:T(1024)(128)(4,1)}), s8[4194304]{0:T(1024)(128)(4,1)S(1)}, s32[]{:S(2)}) async-start(s8[5242880]{0:T(1024)(128)(4,1)} %bitcast.71), calls=%async_computation.6 | async-start | bytes 8388608
  156.9 4.8 %slice-start.1 = ((s8[5242880]{0:T(1024)(128)(4,1)}), s8[1048576]{0:T(1024)(128)(4,1)S(1)}, s32[]{:S(2)}) async-start(s8[5242880]{0:T(1024)(128)(4,1)} %bitcast.71), calls=%async_computation.7 | async-start | bytes 2097152
  161.3 2.4 %slice-start.2 = ((s8[5242880]{0:T(1024)(128)(4,1)}), s8[4194304]{0:T(1024)(128)(4,1)S(1)}, s32[]{:S(2)}) async-start(s8[5242880]{0:T(1024)(128)(4,1)} %bitcast.73), calls=%async_computation.8 | async-start | bytes 8388608
  161.7 2.2 %slice-start.3 = ((s8[5242880]{0:T(1024)(128)(4,1)}), s8[1048576]{0:T(1024)(128)(4,1)S(1)}, s32[]{:S(2)}) async-start(s8[5242880]{0:T(1024)(128)(4,1)} %bitcast.73), calls=%async_computation.9 | async-start | bytes 2097152

commit v2 on v1

v2 whole, which is shorter than its diff:
```python
import math

import jax
import jax.numpy as jnp
from jax import lax
from jax.sharding import Mesh
from jax.sharding import PartitionSpec as P


PLANE = ("xh", "y")
CHIPS = ("xl", "xh", "y")
HIDPLANE = ("xl", "c", "xh", "y")
BF16 = jnp.bfloat16
F32 = jnp.float32


MOVES = (
    ("z", 8, 1, 1),
    ("z", 8, 2, 1),
    ("z", 8, 4, 1),
    ("y", 4, 1, 1),
    ("y", 4, 2, 1),
    ("xh", 2, 1, 1),
    ("xl", 2, 1, 0),
)


def trade(value, axes):
    return lax.all_to_all(value, axes, 0, 0, tiled=True)


def share(value, axes, count):
    return trade(jnp.broadcast_to(value[None], (count,) + value.shape), axes)


def dot_first(left, right):
    return lax.dot_general(left, right, (((0,), (0,)), ((), ())), preferred_element_type=F32)


def dot_last(left, right):
    return lax.dot_general(left, right, (((1,), (1,)), ((), ())), preferred_element_type=F32)


def act_grads(gate_pre, up_pre, hid_grad):
    logistic = jax.nn.sigmoid(gate_pre)
    grad_gate = (hid_grad * up_pre * logistic * (1.0 + gate_pre * (1.0 - logistic))).astype(BF16)
    grad_up = (hid_grad * gate_pre * logistic).astype(BF16)
    return jnp.concatenate([grad_gate, grad_up], axis=1)


def local(
    val_inputs, val_out_grad, w_gate, w_up, w_down, val_attn_inputs, train_inputs, train_grads
):
    feats, units = w_gate.shape
    vals = val_inputs.shape[0]
    n_plane = lax.axis_size(PLANE)
    n_z = lax.axis_size("z")
    n_chips = lax.axis_size(CHIPS)
    n_hidplane = lax.axis_size(HIDPLANE)
    own = units // n_plane
    wide = feats * n_plane

    width = train_inputs.shape[1]
    attn_rows = val_attn_inputs.shape[0]
    chunk = vals // n_hidplane
    rows_z = vals // n_z
    swap = [(0, 1), (1, 0)]
    first_w, first_down = 2 * vals, 2 * vals + 2 * own

    def spread(weight):
        return weight.reshape(feats, n_plane, own)

    def same(value):
        return jnp.broadcast_to(value[:, None], (feats, n_plane, vals))

    row = lax.axis_index(HIDPLANE) * chunk
    attn = val_attn_inputs
    for axis, count, bit, dim in MOVES:
        pairs = [(i, i ^ bit) for i in range(count)]
        theirs = lax.ppermute(attn, axis, pairs)
        high = (lax.axis_index(axis) & bit) != 0
        attn = jnp.concatenate(
            [jnp.where(high, theirs, attn), jnp.where(high, attn, theirs)], axis=dim
        )
    sent = jnp.concatenate(
        [same(val_inputs.T), same(val_out_grad.T), spread(w_gate), spread(w_up), spread(w_down.T)],
        axis=2,
    ).transpose(1, 0, 2)
    got = trade(sent, PLANE).reshape(wide, 3 * own + 2 * vals)
    back_w = got[:, first_w:first_down]
    partial = jnp.concatenate(
        [dot_first(got[:, :vals], back_w), dot_first(got[:, vals:first_w], got[:, first_down:])],
        axis=1,
    ).astype(BF16)
    parts = trade(partial.reshape(n_z, rows_z, 3 * own), "z")
    pre = jnp.sum(parts.astype(F32), axis=0)
    grads = act_grads(pre[:, :own], pre[:, own : 2 * own], pre[:, 2 * own :])
    grads = share(grads, "z", n_z).reshape(vals, 2 * own)
    attn_other = lax.ppermute(attn, "c", swap)
    part = dot_last(grads, back_w)
    parts = trade(part.reshape(n_hidplane, chunk, wide), HIDPLANE)

    gram_own = lax.optimization_barrier(dot_last(train_inputs, attn))
    gram_other = lax.optimization_barrier(dot_last(train_inputs, attn_other))
    dx = jnp.sum(parts, axis=0)
    mine = lax.dynamic_slice_in_dim(got[:, vals:first_w], row, chunk, 1).T
    val_grad = (mine.astype(F32) + dx).astype(BF16)
    val_z = share(val_grad, "z", n_z).reshape(n_z, chunk, n_plane, feats)
    val_z = val_z.transpose(1, 2, 0, 3).reshape(chunk, width)
    val_own = share(val_z, CHIPS, n_chips).reshape(n_chips * chunk, width)
    val_other = lax.ppermute(val_own, "c", swap)
    total = jnp.sum(gram_own * dot_last(train_grads, val_own), axis=1)
    total = total + jnp.sum(gram_other * dot_last(train_grads, val_other), axis=1)
    influence = total / (width * math.sqrt(vals))
    block = lax.dynamic_slice(val_own, (lax.axis_index("xl") * attn_rows, lax.axis_index(("xh", "y", "z")) * feats), (attn_rows, feats))
    return (influence, block)


def solution(mesh):
    fine = Mesh(mesh.devices.reshape(2, 2, 2, 4, 8), ("xl", "c", "xh", "y", "z"))
    tok = ("xh", "y", "z")
    hid = ("xl", "c")
    placed = (
        P(None, tok),
        P(None, tok),
        P(tok, hid),
        P(tok, hid),
        P(hid, tok),
        P(hid, tok),
        P(hid + tok, None),
        P(hid + tok, None),
    )
    return jax.shard_map(
        local,
        mesh=fine,
        in_specs=placed,
        out_specs=(P(hid + tok), P(hid, tok)),
        check_vma=False,
    )
```

time: 167 us -> 170 us (1.018)
  blocking collectives: 79.5 us -> 0 us
  waiting for transfers between devices: 38.9 us -> 82.2 us
  starting transfers between devices: 23.5 us -> 57.5 us
  matrix products: 6.35 us -> 14.4 us
  local copies, waits for them, and re-layouts: 15.2 us -> 9.68 us
  other arithmetic: 1.87 us -> 4.61 us
    all_to_all x3 -> x0, blocking collectives: 79.5 us -> none  [trade(): return lax.all_to_all(value, axes, 0, 0, tiled=True)]
    ppermute x1 -> x9, waiting for transfers between devices: 2.08 us -> 37.6 us  [the longest x7 37.6 us: local(): theirs = lax.ppermute(attn, axis, pairs)]
    ppermute x1 -> x9, starting transfers between devices: 3.35 us -> 20.6 us  [the longest x7 14.6 us: local(): theirs = lax.ppermute(attn, axis, pairs)]
    all_to_all x3 -> x6, starting transfers between devices: 20.1 us -> 37 us  [trade(): return lax.all_to_all(value, axes, 0, 0, tiled=True)]
    dot_general x4 -> x5, matrix products: 5.37 us -> 13.6 us  [dot_last(): lax.dot_general(left, right, (((1,), (1,)), ((), ())), preferred_element_...]
    all_to_all x3 -> x6, waiting for transfers between devices: 36.8 us -> 44.7 us  [trade(): return lax.all_to_all(value, axes, 0, 0, tiled=True)]
    reshape x6 -> x0, local copies, waits for them, and re-layouts: 2.32 us -> none  [the longest x2 1.81 us: rows_of(): val_rows = block[:, :, :width].reshape(n_chips * chunk, width)]
    unnamed x26 -> x16, local copies, waits for them, and re-layouts: 2.08 us -> 0.13 us
  transfers between devices with their start and end apart: 4 -> 15, of which waited for: 4 -> 12; matrix products, arithmetic and copies ran while one was open for 2% -> 9% of each run, Pallas kernels for 0% -> 0%
where the time goes in v2:
time: 170 us; the launch traced here: 169 us
  waiting for transfers between devices  82.2 us (48%)
  starting transfers between devices  57.5 us (34%)
  matrix products  14.4 us (8%)
  local copies, waits for them, and re-layouts  9.68 us (6%)
  other arithmetic  4.61 us (3%)
    all_to_all x6, waiting for transfers between devices, trade(): return lax.all_to_all(value, axes, 0, 0, tiled=True)  44.7 us
    ppermute x7, waiting for transfers between devices, local(): theirs = lax.ppermute(attn, axis, pairs)  37.6 us
    all_to_all x6, starting transfers between devices, trade(): return lax.all_to_all(value, axes, 0, 0, tiled=True)  37 us
    ppermute x7, starting transfers between devices, local(): theirs = lax.ppermute(attn, axis, pairs)  14.6 us
    dot_general x5, matrix products, dot_last(): lax.dot_general(left, right, (((1,), (1,)), ((), ())), preferred_element_...  13.6 us
    ppermute x1, starting transfers between devices, local(): val_other = lax.ppermute(val_own, 'c', swap)  4.08 us
    reshape x6, local copies, waits for them, and re-layouts, spread(): return weight.reshape(feats, n_plane, own)  3.41 us
  transfers between devices with their start and end apart: 15, of which 12 were waited for; matrix products, arithmetic and copies ran while one was open for 9% of the time, Pallas kernels for 0%

profile of v2, /device:TPU:1, one launch (start us, length us, event | category | flops | bytes accessed | tf_op | source)
XLA Modules:
  0.0 169.4 jit_solution(6163040806090358212)
XLA Ops:
  0.7 1.7 %reshape.36 = bf16[64,8,448]{2,1,0:T(8,128)(2,1)S(1)} reshape(bf16[64,3584]{1,0:T(8,128)(2,1)} %param.10) | data formatting | bytes 917504 | tf_op jit(solution)/shard_map/reshape | solution.py:71
  2.4 0.2 copy.41
  2.6 0.6 reshape.37
  3.2 0.2 copy.42
  3.4 0.6 reshape.38
  4.0 0.2 copy.43
  4.2 2.2 %concatenate.43 = bf16[64,8,1856]{2,0,1:T(8,128)(2,1)} concatenate(bf16[64,8,256]{2,0,1:T(8,128)(2,1)S(1)} %broadcast_in_dim.12, bf16[64,8,256]{2,0,1:T(8,128)(2,1)S(1)} %broadcast_in_dim.13, bf16[64,8,448]{2,0,1:T(8,128)(2,1)S(1)} %copy.41, bf16[64,8,448]{2,0,1:T(8,128)(2,1)S(1)} %copy.42, bf16[64,8,448]{2,0,1:T(8,128)(2,1)S(1)} %copy.43), dimensions={2} | concatenate | bytes 3801088 | tf_op jit(solution)/shard_map/concatenate | solution.py:85
  6.4 7.6 %all-to-all-start = ((bf16[8,64,1856]{2,1,0:T(8,128)(2,1)}), bf16[8,64,1856]{2,1,0:T(8,128)(2,1)S(1)}, u32[]{:S(2)}, u32[]{:S(2)}) async-start(bf16[8,64,1856]{2,1,0:T(8,128)(2,1)} %bitcast.4), calls=%async_computation | async-start | bytes 3932160 | tf_op jit(solution)/shard_map/all_to_all | solution.py:29
  14.0 1.7 %collective-permute-start = (bf16[64,64]{1,0:T(8,128)(2,1)S(1)}, bf16[64,64]{1,0:T(8,128)(2,1)S(1)}, u32[]{:S(2)}, u32[]{:S(2)}) collective-permute-start(bf16[64,64]{1,0:T(8,128)(2,1)S(1)} %copy-done.4), channel_id=1, source_target_pairs={{0,1},{1,0},{2,3},{3,2},{4,5},{5,4},{6,7},{7,6},{8,9},{9,8},{10,11... | collective-permute-start | bytes 24584 | tf_op jit(solution)/shard_map/ppermute | solution.py:80
  15.7 1.1 collective-permute-done
  17.0 3.0 %collective-permute-start.1 = (bf16[64,128]{1,0:T(8,128)(2,1)S(1)}, bf16[64,128]{1,0:T(8,128)(2,1)S(1)}, u32[]{:S(2)}, u32[]{:S(2)}) collective-permute-start(bf16[64,128]{1,0:T(8,128)(2,1)S(1)} %pad_maximum_fusion.8), channel_id=1, source_target_pairs={{0,2},{1,3},{2,0},{3,1},{4,6},{5,7},{6,4},{7,5},{8,10},{9,11},{10,... | collective-permute-start | bytes 49160 | tf_op jit(solution)/shard_map/ppermute | solution.py:80
  20.0 1.4 collective-permute-done.1
  21.5 17.3 %all-to-all-done = bf16[8,64,1856]{2,1,0:T(8,128)(2,1)S(1)} async-done(((bf16[8,64,1856]{2,1,0:T(8,128)(2,1)}), bf16[8,64,1856]{2,1,0:T(8,128)(2,1)S(1)}, u32[]{:S(2)}, u32[]{:S(2)}) %all-to-all-start) | async-done | bytes 1900576 | tf_op jit(solution)/shard_map/all_to_all | solution.py:29
  38.8 0.3 convolution_convert_fusion.1
  39.1 0.5 convolution_convert_fusion
  39.8 0.9 pad_maximum_fusion.1
  40.7 8.2 %all-to-all-start.1 = ((bf16[8,32,1344]{2,1,0:T(8,128)(2,1)}), bf16[8,32,1344]{2,1,0:T(8,128)(2,1)S(1)}, u32[]{:S(2)}, u32[]{:S(2)}) async-start(bf16[8,32,1344]{2,1,0:T(8,128)(2,1)} %pad_maximum_fusion.1), calls=%async_computation.1 | async-start | bytes 1441792 | tf_op jit(solution)/shard_map/all_to_all | solution.py:29
  48.9 5.5 %collective-permute-start.2 = (bf16[64,256]{1,0:T(8,128)(2,1)S(1)}, bf16[64,256]{1,0:T(8,128)(2,1)S(1)}, u32[]{:S(2)}, u32[]{:S(2)}) collective-permute-start(bf16[64,256]{1,0:T(8,128)(2,1)S(1)} %pad_maximum_fusion.7), channel_id=1, source_target_pairs={{0,4},{1,5},{2,6},{3,7},{4,0},{5,1},{6,2},{7,3},{8,12},{9,13},{10,... | collective-permute-start | bytes 98312 | tf_op jit(solution)/shard_map/ppermute | solution.py:80
  54.3 18.1 %collective-permute-done.2 = bf16[64,256]{1,0:T(8,128)(2,1)S(1)} collective-permute-done((bf16[64,256]{1,0:T(8,128)(2,1)S(1)}, bf16[64,256]{1,0:T(8,128)(2,1)S(1)}, u32[]{:S(2)}, u32[]{:S(2)}) %collective-permute-start.2) | collective-permute-done | bytes 32800 | tf_op jit(solution)/shard_map/ppermute | solution.py:80
  72.6 3.1 %collective-permute-done.3 = bf16[64,512]{1,0:T(8,128)(2,1)S(1)} collective-permute-done((bf16[64,512]{1,0:T(8,128)(2,1)S(1)}, bf16[64,512]{1,0:T(8,128)(2,1)S(1)}, u32[]{:S(2)}, u32[]{:S(2)}) %collective-permute-start.3) | collective-permute-done | bytes 65568 | tf_op jit(solution)/shard_map/ppermute | solution.py:80
  75.8 5.3 %collective-permute-done.4 = bf16[64,1024]{1,0:T(8,128)(2,1)S(1)} collective-permute-done((bf16[64,1024]{1,0:T(8,128)(2,1)S(1)}, bf16[64,1024]{1,0:T(8,128)(2,1)S(1)}, u32[]{:S(2)}, u32[]{:S(2)}) %collective-permute-start.4) | collective-permute-done | bytes 131104 | tf_op jit(solution)/shard_map/ppermute | solution.py:80
  81.5 0.8 broadcast_in_dim.14
  82.3 3.5 %all-to-all-start.2 = ((bf16[8,32,896]{2,1,0:T(8,128)(2,1)}), bf16[8,32,896]{2,1,0:T(8,128)(2,1)S(1)}, u32[]{:S(2)}, u32[]{:S(2)}) async-start(bf16[8,32,896]{2,1,0:T(8,128)(2,1)} %broadcast_in_dim.14), calls=%async_computation.2 | async-start | bytes 917504 | tf_op jit(solution)/shard_map/all_to_all | solution.py:29
  85.8 2.8 %collective-permute-start.5 = (bf16[64,2048]{1,0:T(8,128)(2,1)S(1)}, bf16[64,2048]{1,0:T(8,128)(2,1)S(1)}, u32[]{:S(2)}, u32[]{:S(2)}) collective-permute-start(bf16[64,2048]{1,0:T(8,128)(2,1)S(1)} %pad_maximum_fusion.3), channel_id=1, source_target_pairs={{0,32},{32,0},{1,33},{33,1},{2,34},{34,2},{3,35},{35,3},{4,36},{36... | collective-permute-start | bytes 786440 | tf_op jit(solution)/shard_map/ppermute | solution.py:80
  88.6 4.0 %collective-permute-done.5 = bf16[64,2048]{1,0:T(8,128)(2,1)S(1)} collective-permute-done((bf16[64,2048]{1,0:T(8,128)(2,1)S(1)}, bf16[64,2048]{1,0:T(8,128)(2,1)S(1)}, u32[]{:S(2)}, u32[]{:S(2)}) %collective-permute-start.5) | collective-permute-done | bytes 262176 | tf_op jit(solution)/shard_map/ppermute | solution.py:80
  92.7 6.0 %all-to-all-done.2 = bf16[8,32,896]{2,1,0:T(8,128)(2,1)S(1)} async-done(((bf16[8,32,896]{2,1,0:T(8,128)(2,1)}), bf16[8,32,896]{2,1,0:T(8,128)(2,1)S(1)}, u32[]{:S(2)}, u32[]{:S(2)}) %all-to-all-start.2) | async-done | bytes 458784 | tf_op jit(solution)/shard_map/all_to_all | solution.py:29
  98.7 1.3 fusion.2
  100.0 9.7 %all-to-all-start.3 = ((f32[32,8,512]{2,1,0:T(8,128)}), f32[32,8,512]{2,1,0:T(8,128)S(1)}, u32[]{:S(2)}, u32[]{:S(2)}) async-start(f32[32,8,512]{2,1,0:T(8,128)} %fusion.2), calls=%async_computation.3 | async-start | bytes 1048576 | tf_op jit(solution)/shard_map/all_to_all | solution.py:29
  109.7 1.5 collective-permute-start.6
  111.4 8.9 %all-to-all-done.3 = f32[32,8,512]{2,1,0:T(8,128)S(1)} async-done(((f32[32,8,512]{2,1,0:T(8,128)}), f32[32,8,512]{2,1,0:T(8,128)S(1)}, u32[]{:S(2)}, u32[]{:S(2)}) %all-to-all-start.3) | async-done | bytes 524320 | tf_op jit(solution)/shard_map/all_to_all | solution.py:29
  120.4 0.6 broadcast_in_dim.15
  121.0 3.3 %all-to-all-start.4 = ((bf16[8,8,512]{2,1,0:T(8,128)(2,1)}), bf16[8,8,512]{2,1,0:T(8,128)(2,1)S(1)}, u32[]{:S(2)}, u32[]{:S(2)}) async-start(bf16[8,8,512]{2,1,0:T(8,128)(2,1)} %broadcast_in_dim.15), calls=%async_computation.4 | async-start | bytes 131072 | tf_op jit(solution)/shard_map/all_to_all | solution.py:29
  124.4 4.5 %collective-permute-done.6 = bf16[64,4096]{1,0:T(8,128)(2,1)} collective-permute-done((bf16[64,4096]{1,0:T(8,128)(2,1)S(1)}, bf16[64,4096]{1,0:T(8,128)(2,1)}, u32[]{:S(2)}, u32[]{:S(2)}) %collective-permute-start.6) | collective-permute-done | bytes 524320 | tf_op jit(solution)/shard_map/ppermute | solution.py:80
  128.8 1.2 broadcast_select_fusion.1
  130.1 1.6 all-to-all-done.4
  131.8 0.2 broadcast_in_dim.16
  132.0 1.1 broadcast_in_dim.17
  133.1 4.7 %all-to-all-start.5 = ((bf16[16,8,4096]{2,1,0:T(8,128)(2,1)}), bf16[16,8,4096]{2,1,0:T(8,128)(2,1)S(1)}, u32[]{:S(2)}, u32[]{:S(2)}) async-start(bf16[16,8,4096]{2,1,0:T(8,128)(2,1)} %broadcast_in_dim.17), calls=%async_computation.5 | async-start | bytes 2097152 | tf_op jit(solution)/shard_map/all_to_all | solution.py:29
  137.9 1.0 pad_maximum_fusion
  138.9 1.9 %collective-permute-start.7 = (bf16[128,4096]{1,0:T(8,128)(2,1)}, bf16[128,4096]{1,0:T(8,128)(2,1)}, u32[]{:S(2)}, u32[]{:S(2)}) collective-permute-start(bf16[128,4096]{1,0:T(8,128)(2,1)} %pad_maximum_fusion), channel_id=1, source_target_pairs={{0,64},{64,0},{1,65},{65,1},{2,66},{66,2},{3,67},{67,3},{4,68},{68... | collective-permute-start | bytes 3145736 | tf_op jit(solution)/shard_map/ppermute | solution.py:99
  140.7 10.9 %all-to-all-done.5 = bf16[16,8,4096]{2,1,0:T(8,128)(2,1)S(1)} async-done(((bf16[16,8,4096]{2,1,0:T(8,128)(2,1)}), bf16[16,8,4096]{2,1,0:T(8,128)(2,1)S(1)}, u32[]{:S(2)}, u32[]{:S(2)}) %all-to-all-start.5) | async-done | bytes 1048608 | tf_op jit(solution)/shard_map/all_to_all | solution.py:29
  151.7 4.1 %collective-permute-start.8 = (bf16[128,4096]{1,0:T(8,128)(2,1)S(1)}, bf16[128,4096]{1,0:T(8,128)(2,1)S(1)}, u32[]{:S(2)}, u32[]{:S(2)}) collective-permute-start(bf16[128,4096]{1,0:T(8,128)(2,1)S(1)} %bitcast.46), channel_id=1, source_target_pairs={{0,64},{64,0},{1,65},{65,1},{2,66},{66,2},{3,67},{67,3},{4,68},{68... | collective-permute-start | bytes 3145736 | tf_op jit(solution)/shard_map/ppermute | solution.py:111
  155.8 4.2 %convolution_bitcast_fusion.3 = f32[640,128]{0,1:T(8,128)S(1)} fusion(bf16[640,4096]{1,0:T(8,128)(2,1)} %param.14, bf16[64,4096]{1,0:T(8,128)(2,1)S(1)} %get-tuple-element.3, bf16[64,4096]{1,0:T(8,128)(2,1)S(1)} %get-tuple-element.2), kind=kOutput, calls=%fused_computation.7 | convolution fusion | flops 673185792 | bytes 6619136 | tf_op jit(solution)/shard_map/dot_general | solution.py:41
  160.0 4.6 %convolution_bitcast_fusion.1 = f32[640,128]{0,1:T(8,128)S(1)} fusion(bf16[128,4096]{1,0:T(8,128)(2,1)} %collective-permute-done.7, bf16[640,4096]{1,0:T(8,128)(2,1)} %param.14), kind=kOutput, calls=%fused_computation.4 | convolution fusion | flops 671088640 | bytes 6619136 | tf_op jit(solution)/shard_map/dot_general | solution.py:41
  164.6 0.7 dynamic_slice.7
  165.3 1.8 %fusion.1 = f32[640]{0:T(1024)S(1)} fusion(f32[640,128]{0,1:T(8,128)S(1)} %convolution_bitcast_fusion.3, bf16[640,4096]{1,0:T(8,128)(2,1)S(1)} %bitcast.41, bf16[16,8,4096]{2,1,0:T(8,128)(2,1)S(1)} %all-to-all-done.5), kind=kOutput, calls=%fused_computation.8 | convolution fusion | flops 671251840 | bytes 6621696 | tf_op jit(solution)/shard_map/dot_general | solution.py:41
  167.0 1.7 %convolution_bitcast_fusion = f32[640,128]{0,1:T(8,128)S(1)} fusion(bf16[128,4096]{1,0:T(8,128)(2,1)S(1)} %collective-permute-done.8, bf16[640,4096]{1,0:T(8,128)(2,1)S(1)} %bitcast.41), kind=kOutput, calls=%fused_computation.3 | convolution fusion | flops 671088640 | bytes 6619136 | tf_op jit(solution)/shard_map/dot_general | solution.py:41
  168.8 0.6 add_multiply_fusion
  (46 shorter events, 1.6 us)
Async XLA Ops:
  0.6 1.9 %copy-start = (bf16[64,3584]{1,0:T(8,128)(2,1)S(1)}, bf16[64,3584]{1,0:T(8,128)(2,1)}, u32[]{:S(2)}) copy-start(bf16[64,3584]{1,0:T(8,128)(2,1)} %param.11) | copy-start | bytes 1376260
  0.6 2.7 %copy-start.1 = (bf16[3584,64]{0,1:T(8,128)(2,1)S(1)}, bf16[3584,64]{0,1:T(8,128)(2,1)}, u32[]{:S(2)}) copy-start(bf16[3584,64]{0,1:T(8,128)(2,1)} %param.12) | copy-start | bytes 1376260
  2.5 1.6 copy-start.2
  2.5 1.6 copy-start.3
  6.4 7.6 %copy-start.4 = (bf16[64,64]{1,0:T(8,128)(2,1)S(1)}, bf16[64,64]{1,0:T(8,128)(2,1)}, u32[]{:S(2)}) copy-start(bf16[64,64]{1,0:T(8,128)(2,1)} %param.13) | copy-start | bytes 24580
  6.4 32.4 %all-to-all-start = ((bf16[8,64,1856]{2,1,0:T(8,128)(2,1)}), bf16[8,64,1856]{2,1,0:T(8,128)(2,1)S(1)}, u32[]{:S(2)}, u32[]{:S(2)}) async-start(bf16[8,64,1856]{2,1,0:T(8,128)(2,1)} %bitcast.4), calls=%async_computation | async-start | bytes 3932160 | tf_op jit(solution)/shard_map/all_to_all | solution.py:29
  14.0 2.9 %collective-permute-start = (bf16[64,64]{1,0:T(8,128)(2,1)S(1)}, bf16[64,64]{1,0:T(8,128)(2,1)S(1)}, u32[]{:S(2)}, u32[]{:S(2)}) collective-permute-start(bf16[64,64]{1,0:T(8,128)(2,1)S(1)} %copy-done.4), channel_id=1, source_target_pairs={{0,1},{1,0},{2,3},{3,2},{4,5},{5,4},{6,7},{7,6},{8,9},{9,8},{10,11... | collective-permute-start | bytes 24584 | tf_op jit(solution)/shard_map/ppermute | solution.py:80
  17.0 4.4 %collective-permute-start.1 = (bf16[64,128]{1,0:T(8,128)(2,1)S(1)}, bf16[64,128]{1,0:T(8,128)(2,1)S(1)}, u32[]{:S(2)}, u32[]{:S(2)}) collective-permute-start(bf16[64,128]{1,0:T(8,128)(2,1)S(1)} %pad_maximum_fusion.8), channel_id=1, source_target_pairs={{0,2},{1,3},{2,0},{3,1},{4,6},{5,7},{6,4},{7,5},{8,10},{9,11},{10,... | collective-permute-start | bytes 49160 | tf_op jit(solution)/shard_map/ppermute | solution.py:80
  40.7 40.5 %all-to-all-start.1 = ((bf16[8,32,1344]{2,1,0:T(8,128)(2,1)}), bf16[8,32,1344]{2,1,0:T(8,128)(2,1)S(1)}, u32[]{:S(2)}, u32[]{:S(2)}) async-start(bf16[8,32,1344]{2,1,0:T(8,128)(2,1)} %pad_maximum_fusion.1), calls=%async_computation.1 | async-start | bytes 1441792 | tf_op jit(solution)/shard_map/all_to_all | solution.py:29
  48.9 23.6 %collective-permute-start.2 = (bf16[64,256]{1,0:T(8,128)(2,1)S(1)}, bf16[64,256]{1,0:T(8,128)(2,1)S(1)}, u32[]{:S(2)}, u32[]{:S(2)}) collective-permute-start(bf16[64,256]{1,0:T(8,128)(2,1)S(1)} %pad_maximum_fusion.7), channel_id=1, source_target_pairs={{0,4},{1,5},{2,6},{3,7},{4,0},{5,1},{6,2},{7,3},{8,12},{9,13},{10,... | collective-permute-start | bytes 98312 | tf_op jit(solution)/shard_map/ppermute | solution.py:80
  72.5 3.2 %collective-permute-start.3 = (bf16[64,512]{1,0:T(8,128)(2,1)S(1)}, bf16[64,512]{1,0:T(8,128)(2,1)S(1)}, u32[]{:S(2)}, u32[]{:S(2)}) collective-permute-start(bf16[64,512]{1,0:T(8,128)(2,1)S(1)} %pad_maximum_fusion.5), channel_id=1, source_target_pairs={{0,8},{8,0},{16,24},{24,16},{1,9},{9,1},{17,25},{25,17},{2,10},{10... | collective-permute-start | bytes 196616 | tf_op jit(solution)/shard_map/ppermute | solution.py:80
  75.7 5.4 %collective-permute-start.4 = (bf16[64,1024]{1,0:T(8,128)(2,1)S(1)}, bf16[64,1024]{1,0:T(8,128)(2,1)S(1)}, u32[]{:S(2)}, u32[]{:S(2)}) collective-permute-start(bf16[64,1024]{1,0:T(8,128)(2,1)S(1)} %pad_maximum_fusion.4), channel_id=1, source_target_pairs={{0,16},{8,24},{16,0},{24,8},{1,17},{9,25},{17,1},{25,9},{2,18},{10... | collective-permute-start | bytes 393224 | tf_op jit(solution)/shard_map/ppermute | solution.py:80
  82.3 16.4 %all-to-all-start.2 = ((bf16[8,32,896]{2,1,0:T(8,128)(2,1)}), bf16[8,32,896]{2,1,0:T(8,128)(2,1)S(1)}, u32[]{:S(2)}, u32[]{:S(2)}) async-start(bf16[8,32,896]{2,1,0:T(8,128)(2,1)} %broadcast_in_dim.14), calls=%async_computation.2 | async-start | bytes 917504 | tf_op jit(solution)/shard_map/all_to_all | solution.py:29
  85.8 6.8 %collective-permute-start.5 = (bf16[64,2048]{1,0:T(8,128)(2,1)S(1)}, bf16[64,2048]{1,0:T(8,128)(2,1)S(1)}, u32[]{:S(2)}, u32[]{:S(2)}) collective-permute-start(bf16[64,2048]{1,0:T(8,128)(2,1)S(1)} %pad_maximum_fusion.3), channel_id=1, source_target_pairs={{0,32},{32,0},{1,33},{33,1},{2,34},{34,2},{3,35},{35,3},{4,36},{36... | collective-permute-start | bytes 786440 | tf_op jit(solution)/shard_map/ppermute | solution.py:80
  100.0 20.3 %all-to-all-start.3 = ((f32[32,8,512]{2,1,0:T(8,128)}), f32[32,8,512]{2,1,0:T(8,128)S(1)}, u32[]{:S(2)}, u32[]{:S(2)}) async-start(f32[32,8,512]{2,1,0:T(8,128)} %fusion.2), calls=%async_computation.3 | async-start | bytes 1048576 | tf_op jit(solution)/shard_map/all_to_all | solution.py:29
  109.7 19.1 %collective-permute-start.6 = (bf16[64,4096]{1,0:T(8,128)(2,1)S(1)}, bf16[64,4096]{1,0:T(8,128)(2,1)}, u32[]{:S(2)}, u32[]{:S(2)}) collective-permute-start(bf16[64,4096]{1,0:T(8,128)(2,1)S(1)} %pad_maximum_fusion.2), channel_id=1, source_target_pairs={{0,128},{128,0},{1,129},{129,1},{2,130},{130,2},{3,131},{131,3},{4... | collective-permute-start | bytes 1572872 | tf_op jit(solution)/shard_map/ppermute | solution.py:80
  121.0 10.6 %all-to-all-start.4 = ((bf16[8,8,512]{2,1,0:T(8,128)(2,1)}), bf16[8,8,512]{2,1,0:T(8,128)(2,1)S(1)}, u32[]{:S(2)}, u32[]{:S(2)}) async-start(bf16[8,8,512]{2,1,0:T(8,128)(2,1)} %broadcast_in_dim.15), calls=%async_computation.4 | async-start | bytes 131072 | tf_op jit(solution)/shard_map/all_to_all | solution.py:29
  133.1 18.5 %all-to-all-start.5 = ((bf16[16,8,4096]{2,1,0:T(8,128)(2,1)}), bf16[16,8,4096]{2,1,0:T(8,128)(2,1)S(1)}, u32[]{:S(2)}, u32[]{:S(2)}) async-start(bf16[16,8,4096]{2,1,0:T(8,128)(2,1)} %broadcast_in_dim.17), calls=%async_computation.5 | async-start | bytes 2097152 | tf_op jit(solution)/shard_map/all_to_all | solution.py:29
  137.8 27.4 %slice-start = ((s8[5242880]{0:T(1024)(128)(4,1)}), s8[1048576]{0:T(1024)(128)(4,1)S(1)}, s32[]{:S(2)}) async-start(s8[5242880]{0:T(1024)(128)(4,1)} %bitcast.40), calls=%async_computation.6 | async-start | bytes 2097152
  138.9 21.1 %collective-permute-start.7 = (bf16[128,4096]{1,0:T(8,128)(2,1)}, bf16[128,4096]{1,0:T(8,128)(2,1)}, u32[]{:S(2)}, u32[]{:S(2)}) collective-permute-start(bf16[128,4096]{1,0:T(8,128)(2,1)} %pad_maximum_fusion), channel_id=1, source_target_pairs={{0,64},{64,0},{1,65},{65,1},{2,66},{66,2},{3,67},{67,3},{4,68},{68... | collective-permute-start | bytes 3145736 | tf_op jit(solution)/shard_map/ppermute | solution.py:99
  151.7 13.6 %slice-start.1 = ((s8[5242880]{0:T(1024)(128)(4,1)}), s8[4194304]{0:T(1024)(128)(4,1)S(1)}, s32[]{:S(2)}) async-start(s8[5242880]{0:T(1024)(128)(4,1)} %bitcast.40), calls=%async_computation.7 | async-start | bytes 8388608
  151.7 15.4 %collective-permute-start.8 = (bf16[128,4096]{1,0:T(8,128)(2,1)S(1)}, bf16[128,4096]{1,0:T(8,128)(2,1)S(1)}, u32[]{:S(2)}, u32[]{:S(2)}) collective-permute-start(bf16[128,4096]{1,0:T(8,128)(2,1)S(1)} %bitcast.46), channel_id=1, source_target_pairs={{0,64},{64,0},{1,65},{65,1},{2,66},{66,2},{3,67},{67,3},{4,68},{68... | collective-permute-start | bytes 3145736 | tf_op jit(solution)/shard_map/ppermute | solution.py:111

commit v3 on v2

--- a/solution.py
+++ b/solution.py
@@ -1,8 +1,11 @@
+import functools
 import math
 
 import jax
 import jax.numpy as jnp
 from jax import lax
+from jax.experimental import pallas as pl
+from jax.experimental.pallas import tpu as pltpu
 from jax.sharding import Mesh
 from jax.sharding import PartitionSpec as P
 
@@ -39,6 +42,89 @@
 
 def dot_last(left, right):
     return lax.dot_general(left, right, (((1,), (1,)), ((), ())), preferred_element_type=F32)
+
+
+def pack_kernel(in_ref, grad_ref, gate_ref, up_ref, down_ref, out_ref, held, sems):
+    vals = in_ref.shape[1]
+    own = (out_ref.shape[2] - 2 * vals) // 3
+    copies = []
+    for peer in range(out_ref.shape[0]):
+        here = slice(peer * own, (peer + 1) * own)
+        held[peer, :, :vals] = in_ref[...]
+        held[peer, :, vals : 2 * vals] = grad_ref[...]
+        start = 2 * vals
+        for ref in (gate_ref, up_ref, down_ref):
+            held[peer, :, start : start + own] = ref[:, here]
+            start += own
+        copies.append(pltpu.make_async_copy(held.at[peer], out_ref.at[peer], sems.at[peer]))
+        copies[-1].start()
+    for copy in copies:
+        copy.wait()
+
+
+def pack(inputs_t, out_grad_t, w_gate, w_up, w_down_t, peers):
+    feats, vals = inputs_t.shape
+    shape = (peers, feats, 2 * vals + 3 * (w_gate.shape[1] // peers))
+    return pl.pallas_call(
+        pack_kernel,
+        out_specs=pl.BlockSpec(memory_space=pl.ANY),
+        out_shape=jax.ShapeDtypeStruct(shape, BF16),
+        scratch_shapes=[pltpu.VMEM(shape, BF16), pltpu.SemaphoreType.DMA((peers,))],
+        name="pack",
+    )(inputs_t, out_grad_t, w_gate, w_up, w_down_t)
+
+
+def gram_kernel(train_ref, val_ref, out_ref):
+    out_ref[...] = dot_last(val_ref[...], train_ref[...])
+
+
+def gram(train, val):
+    tokens, width = train.shape
+    rows = val.shape[0]
+    block = 128
+    return pl.pallas_call(
+        gram_kernel,
+        grid=(tokens // block,),
+        in_specs=[
+            pl.BlockSpec((block, width), lambda i: (i, 0)),
+            pl.BlockSpec((rows, width), lambda i: (0, 0)),
+        ],
+        out_specs=pl.BlockSpec((rows, block), lambda i: (0, i)),
+        out_shape=jax.ShapeDtypeStruct((rows, tokens), F32),
+        compiler_params=pltpu.CompilerParams(vmem_limit_bytes=10 * 1024 * 1024),
+        name="gram",
+    )(train, val)
+
+
+def pair_kernel(scale, train_ref, own_ref, other_ref, gram_own_ref, gram_other_ref, out_ref, block_ref):
+    rows, feats = block_ref.shape
+    tile = (lax.axis_index("xh") * 4 + lax.axis_index("y")) * 8 + lax.axis_index("z")
+    row = pl.multiple_of(lax.axis_index("xl") * rows, rows)
+    col = pl.multiple_of((tile // 2) * (2 * feats), 2 * feats)
+    found = own_ref[pl.ds(row, rows), pl.ds(col, 2 * feats)].astype(F32)
+    half = jnp.where(tile % 2 == 0, found[:, :feats], found[:, feats:])
+    block_ref[...] = half.astype(BF16)
+    val = jnp.concatenate([own_ref[...], other_ref[...]], axis=0)
+    grad_gram = dot_last(val, train_ref[...])
+    count = own_ref.shape[0]
+    total = gram_own_ref[...] * grad_gram[:count] + gram_other_ref[...] * grad_gram[count:]
+    total = jnp.sum(total, axis=0, keepdims=True) * scale
+    out_ref[...] = total.reshape(out_ref.shape)
+
+
+def pair_values(scale, train, own, other, gram_own, gram_other, rows, feats):
+    vmem = pl.BlockSpec(memory_space=pltpu.VMEM)
+    return pl.pallas_call(
+        functools.partial(pair_kernel, scale),
+        out_shape=(
+            jax.ShapeDtypeStruct((train.shape[0],), F32),
+            jax.ShapeDtypeStruct((rows, feats), BF16),
+        ),
+        in_specs=[vmem] * 5,
+        out_specs=(vmem, vmem),
+        compiler_params=pltpu.CompilerParams(vmem_limit_bytes=24 * 1024 * 1024),
+        name="pair_values",
+    )(train, own, other, gram_own, gram_other)
 
 
 def act_grads(gate_pre, up_pre, hid_grad):
@@ -67,12 +153,6 @@
     swap = [(0, 1), (1, 0)]
     first_w, first_down = 2 * vals, 2 * vals + 2 * own
 
-    def spread(weight):
-        return weight.reshape(feats, n_plane, own)
-
-    def same(value):
-        return jnp.broadcast_to(value[:, None], (feats, n_plane, vals))
-
     row = lax.axis_index(HIDPLANE) * chunk
     attn = val_attn_inputs
     for axis, count, bit, dim in MOVES:
@@ -82,10 +162,7 @@
         attn = jnp.concatenate(
             [jnp.where(high, theirs, attn), jnp.where(high, attn, theirs)], axis=dim
         )
-    sent = jnp.concatenate(
-        [same(val_inputs.T), same(val_out_grad.T), spread(w_gate), spread(w_up), spread(w_down.T)],
-        axis=2,
-    ).transpose(1, 0, 2)
+    sent = pack(val_inputs.T, val_out_grad.T, w_gate, w_up, w_down.T, n_plane)
     got = trade(sent, PLANE).reshape(wide, 3 * own + 2 * vals)
     back_w = got[:, first_w:first_down]
     partial = jnp.concatenate(
@@ -100,19 +177,20 @@
     part = dot_last(grads, back_w)
     parts = trade(part.reshape(n_hidplane, chunk, wide), HIDPLANE)
 
-    gram_own = lax.optimization_barrier(dot_last(train_inputs, attn))
-    gram_other = lax.optimization_barrier(dot_last(train_inputs, attn_other))
+    gram_own = gram(train_inputs, attn)
+    gram_other = gram(train_inputs, attn_other)
     dx = jnp.sum(parts, axis=0)
     mine = lax.dynamic_slice_in_dim(got[:, vals:first_w], row, chunk, 1).T
+    mine = lax.optimization_barrier(mine)
     val_grad = (mine.astype(F32) + dx).astype(BF16)
     val_z = share(val_grad, "z", n_z).reshape(n_z, chunk, n_plane, feats)
     val_z = val_z.transpose(1, 2, 0, 3).reshape(chunk, width)
     val_own = share(val_z, CHIPS, n_chips).reshape(n_chips * chunk, width)
     val_other = lax.ppermute(val_own, "c", swap)
-    total = jnp.sum(gram_own * dot_last(train_grads, val_own), axis=1)
-    total = total + jnp.sum(gram_other * dot_last(train_grads, val_other), axis=1)
-    influence = total / (width * math.sqrt(vals))
-    block = lax.dynamic_slice(val_own, (lax.axis_index("xl") * attn_rows, lax.axis_index(("xh", "y", "z")) * feats), (attn_rows, feats))
+    scale = 1.0 / (width * math.sqrt(vals))
+    influence, block = pair_values(
+        scale, train_grads, val_own, val_other, gram_own, gram_other, attn_rows, feats
+    )
     return (influence, block)
 
 

time: 170 us -> 165 us (0.971)
  matrix products: 14.4 us -> 2.07 us
  Pallas kernels: 0 us -> 9.82 us
  other arithmetic: 4.61 us -> 2.78 us
    dot_general x5 -> x1, matrix products: 13.6 us -> 1.27 us  [dot_last(): lax.dot_general(left, right, (((1,), (1,)), ((), ())), preferred_element_...]
    pallas_call x0 -> x4, Pallas kernels: none -> 9.82 us  [the longest x2 4.62 us: gram(): pl.pallas_call(gram_kernel, grid=(tokens // block,), in_specs=[pl.BlockSp...]
    all_to_all x6, waiting for transfers between devices: 44.7 us -> 50 us  [trade(): return lax.all_to_all(value, axes, 0, 0, tiled=True)]
    unnamed x16 -> x8, local copies, waits for them, and re-layouts: 0.13 us -> 5.06 us
    ppermute x7, waiting for transfers between devices: 37.6 us -> 33.1 us  [local(): theirs = lax.ppermute(attn, axis, pairs)]
    reshape x6 -> x0, local copies, waits for them, and re-layouts: 3.41 us -> none  [spread(): return weight.reshape(feats, n_plane, own)]
    concatenate x1 -> x0, local copies, waits for them, and re-layouts: 2.18 us -> none  [local(): jnp.concatenate([same(val_inputs.T), same(val_out_grad.T), spread(w_gate)...]
  transfers between devices with their start and end apart: 15 -> 15, of which waited for: 12 -> 11; matrix products, arithmetic and copies ran while one was open for 9% -> 2% of each run, Pallas kernels for 0% -> 3%
where the time goes in v3:
time: 165 us
  waiting for transfers between devices  83.2 us (50%)
  starting transfers between devices  57.6 us (35%)
  Pallas kernels  9.82 us (6%)
  local copies, waits for them, and re-layouts  8.29 us (5%)
  other arithmetic  2.78 us (2%)
  matrix products  2.07 us (1%)
    all_to_all x6, waiting for transfers between devices, trade(): return lax.all_to_all(value, axes, 0, 0, tiled=True)  50 us
    all_to_all x6, starting transfers between devices, trade(): return lax.all_to_all(value, axes, 0, 0, tiled=True)  36.7 us
    ppermute x7, waiting for transfers between devices, local(): theirs = lax.ppermute(attn, axis, pairs)  33.1 us
    ppermute x7, starting transfers between devices, local(): theirs = lax.ppermute(attn, axis, pairs)  14.6 us
    unnamed x8, local copies, waits for them, and re-layouts  5.06 us
    pallas_call x2, Pallas kernels, gram(): pl.pallas_call(gram_kernel, grid=(tokens // block,), in_specs=[pl.BlockSp...  4.62 us
    ppermute x1, starting transfers between devices, local(): val_other = lax.ppermute(val_own, 'c', swap)  4.23 us
  transfers between devices with their start and end apart: 15, of which 11 were waited for; matrix products, arithmetic and copies ran while one was open for 2% of the time, Pallas kernels for 3%

profile of v3, /device:TPU:1, one launch (start us, length us, event | category | flops | bytes accessed | tf_op | source)
XLA Modules:
  0.0 164.6 jit_solution(3980509675569856493)
XLA Ops:
  0.6 2.8 %pack.1 = bf16[8,64,1856]{2,1,0:T(8,128)(2,1)} custom-call(bf16[64,256]{1,0:T(8,128)(2,1)} %bitcast.28, bf16[64,256]{1,0:T(8,128)(2,1)} %bitcast.29, bf16[64,3584]{1,0:T(8,128)(2,1)} %gate_ref.1, bf16[64,3584]{1,0:T(8,128)(2,1)} %up_ref.1, bf16[64,3584]{1,0:T(8,128)(2,1)} %bitcast.26), custom_call_target="tpu_custom_call" | custom-call | tf_op jit(solution)/shard_map/pack/pallas_call | solution.py:68
  3.4 7.5 %all-to-all-start = ((bf16[8,64,1856]{2,1,0:T(8,128)(2,1)}), bf16[8,64,1856]{2,1,0:T(8,128)(2,1)S(1)}, u32[]{:S(2)}, u32[]{:S(2)}) async-start(bf16[8,64,1856]{2,1,0:T(8,128)(2,1)} %pack.1), calls=%async_computation | async-start | bytes 3932160 | tf_op jit(solution)/shard_map/all_to_all | solution.py:32
  10.9 1.7 %collective-permute-start.1 = (bf16[64,64]{1,0:T(8,128)(2,1)S(1)}, bf16[64,64]{1,0:T(8,128)(2,1)S(1)}, u32[]{:S(2)}, u32[]{:S(2)}) collective-permute-start(bf16[64,64]{1,0:T(8,128)(2,1)S(1)} %copy-done.2), channel_id=1, source_target_pairs={{0,1},{1,0},{2,3},{3,2},{4,5},{5,4},{6,7},{7,6},{8,9},{9,8},{10,11... | collective-permute-start | bytes 24584 | tf_op jit(solution)/shard_map/ppermute | solution.py:160
  12.6 1.1 collective-permute-done.1
  13.9 3.0 %collective-permute-start.2 = (bf16[64,128]{1,0:T(8,128)(2,1)S(1)}, bf16[64,128]{1,0:T(8,128)(2,1)S(1)}, u32[]{:S(2)}, u32[]{:S(2)}) collective-permute-start(bf16[64,128]{1,0:T(8,128)(2,1)S(1)} %pad_maximum_fusion.8), channel_id=1, source_target_pairs={{0,2},{1,3},{2,0},{3,1},{4,6},{5,7},{6,4},{7,5},{8,10},{9,11},{10,... | collective-permute-start | bytes 49160 | tf_op jit(solution)/shard_map/ppermute | solution.py:160
  16.9 1.4 collective-permute-done.2
  18.4 17.3 %all-to-all-done = bf16[8,64,1856]{2,1,0:T(8,128)(2,1)S(1)} async-done(((bf16[8,64,1856]{2,1,0:T(8,128)(2,1)}), bf16[8,64,1856]{2,1,0:T(8,128)(2,1)S(1)}, u32[]{:S(2)}, u32[]{:S(2)}) %all-to-all-start) | async-done | bytes 1900576 | tf_op jit(solution)/shard_map/all_to_all | solution.py:32
  35.7 0.3 convolution_convert_fusion.1
  36.1 0.5 convolution_convert_fusion
  36.5 0.1 copy.21
  36.7 0.9 pad_maximum_fusion.1
  37.6 8.2 %all-to-all-start.1 = ((bf16[8,32,1344]{2,1,0:T(8,128)(2,1)}), bf16[8,32,1344]{2,1,0:T(8,128)(2,1)S(1)}, u32[]{:S(2)}, u32[]{:S(2)}) async-start(bf16[8,32,1344]{2,1,0:T(8,128)(2,1)} %pad_maximum_fusion.1), calls=%async_computation.1 | async-start | bytes 1441792 | tf_op jit(solution)/shard_map/all_to_all | solution.py:32
  45.8 5.5 %collective-permute-start.3 = (bf16[64,256]{1,0:T(8,128)(2,1)S(1)}, bf16[64,256]{1,0:T(8,128)(2,1)S(1)}, u32[]{:S(2)}, u32[]{:S(2)}) collective-permute-start(bf16[64,256]{1,0:T(8,128)(2,1)S(1)} %pad_maximum_fusion.7), channel_id=1, source_target_pairs={{0,4},{1,5},{2,6},{3,7},{4,0},{5,1},{6,2},{7,3},{8,12},{9,13},{10,... | collective-permute-start | bytes 98312 | tf_op jit(solution)/shard_map/ppermute | solution.py:160
  51.3 18.1 %collective-permute-done.3 = bf16[64,256]{1,0:T(8,128)(2,1)S(1)} collective-permute-done((bf16[64,256]{1,0:T(8,128)(2,1)S(1)}, bf16[64,256]{1,0:T(8,128)(2,1)S(1)}, u32[]{:S(2)}, u32[]{:S(2)}) %collective-permute-start.3) | collective-permute-done | bytes 32800 | tf_op jit(solution)/shard_map/ppermute | solution.py:160
  69.4 0.1 collective-permute-start.4
  69.5 3.1 %collective-permute-done.4 = bf16[64,512]{1,0:T(8,128)(2,1)S(1)} collective-permute-done((bf16[64,512]{1,0:T(8,128)(2,1)S(1)}, bf16[64,512]{1,0:T(8,128)(2,1)S(1)}, u32[]{:S(2)}, u32[]{:S(2)}) %collective-permute-start.4) | collective-permute-done | bytes 65568 | tf_op jit(solution)/shard_map/ppermute | solution.py:160
  72.6 0.1 collective-permute-start.5
  72.8 5.3 %collective-permute-done.5 = bf16[64,1024]{1,0:T(8,128)(2,1)S(1)} collective-permute-done((bf16[64,1024]{1,0:T(8,128)(2,1)S(1)}, bf16[64,1024]{1,0:T(8,128)(2,1)S(1)}, u32[]{:S(2)}, u32[]{:S(2)}) %collective-permute-start.5) | collective-permute-done | bytes 131104 | tf_op jit(solution)/shard_map/ppermute | solution.py:160
  78.1 0.1 convert_reduce_fusion
  78.2 0.1 fusion.8
  78.4 0.8 broadcast_in_dim.8
  79.2 3.5 %all-to-all-start.2 = ((bf16[8,32,896]{2,1,0:T(8,128)(2,1)}), bf16[8,32,896]{2,1,0:T(8,128)(2,1)S(1)}, u32[]{:S(2)}, u32[]{:S(2)}) async-start(bf16[8,32,896]{2,1,0:T(8,128)(2,1)} %broadcast_in_dim.8), calls=%async_computation.2 | async-start | bytes 917504 | tf_op jit(solution)/shard_map/all_to_all | solution.py:32
  82.7 2.8 %collective-permute-start.6 = (bf16[64,2048]{1,0:T(8,128)(2,1)S(1)}, bf16[64,2048]{1,0:T(8,128)(2,1)S(1)}, u32[]{:S(2)}, u32[]{:S(2)}) collective-permute-start(bf16[64,2048]{1,0:T(8,128)(2,1)S(1)} %pad_maximum_fusion.3), channel_id=1, source_target_pairs={{0,32},{32,0},{1,33},{33,1},{2,34},{34,2},{3,35},{35,3},{4,36},{36... | collective-permute-start | bytes 786440 | tf_op jit(solution)/shard_map/ppermute | solution.py:160
  85.5 4.0 %collective-permute-done.6 = bf16[64,2048]{1,0:T(8,128)(2,1)S(1)} collective-permute-done((bf16[64,2048]{1,0:T(8,128)(2,1)S(1)}, bf16[64,2048]{1,0:T(8,128)(2,1)S(1)}, u32[]{:S(2)}, u32[]{:S(2)}) %collective-permute-start.6) | collective-permute-done | bytes 262176 | tf_op jit(solution)/shard_map/ppermute | solution.py:160
  89.5 0.1 broadcast_select_fusion.3
  89.6 6.0 %all-to-all-done.2 = bf16[8,32,896]{2,1,0:T(8,128)(2,1)S(1)} async-done(((bf16[8,32,896]{2,1,0:T(8,128)(2,1)}), bf16[8,32,896]{2,1,0:T(8,128)(2,1)S(1)}, u32[]{:S(2)}, u32[]{:S(2)}) %all-to-all-start.2) | async-done | bytes 458784 | tf_op jit(solution)/shard_map/all_to_all | solution.py:32
  95.6 1.3 fusion
  96.9 9.7 %all-to-all-start.3 = ((f32[32,8,512]{2,1,0:T(8,128)}), f32[32,8,512]{2,1,0:T(8,128)S(1)}, u32[]{:S(2)}, u32[]{:S(2)}) async-start(f32[32,8,512]{2,1,0:T(8,128)} %fusion), calls=%async_computation.3 | async-start | bytes 1048576 | tf_op jit(solution)/shard_map/all_to_all | solution.py:32
  106.6 0.9 pad_maximum_fusion.2
  107.4 1.4 collective-permute-start.7
  108.9 0.1 constant_dynamic-slice_fusion
  109.0 8.2 %all-to-all-done.3 = f32[32,8,512]{2,1,0:T(8,128)S(1)} async-done(((f32[32,8,512]{2,1,0:T(8,128)}), f32[32,8,512]{2,1,0:T(8,128)S(1)}, u32[]{:S(2)}, u32[]{:S(2)}) %all-to-all-start.3) | async-done | bytes 524320 | tf_op jit(solution)/shard_map/all_to_all | solution.py:32
  117.3 0.6 broadcast_in_dim.9
  117.9 3.3 %all-to-all-start.4 = ((bf16[8,8,512]{2,1,0:T(8,128)(2,1)}), bf16[8,8,512]{2,1,0:T(8,128)(2,1)S(1)}, u32[]{:S(2)}, u32[]{:S(2)}) async-start(bf16[8,8,512]{2,1,0:T(8,128)(2,1)} %broadcast_in_dim.9), calls=%async_computation.4 | async-start | bytes 131072 | tf_op jit(solution)/shard_map/all_to_all | solution.py:32
  121.3 7.2 %all-to-all-done.4 = bf16[8,8,512]{2,1,0:T(8,128)(2,1)S(1)} async-done(((bf16[8,8,512]{2,1,0:T(8,128)(2,1)}), bf16[8,8,512]{2,1,0:T(8,128)(2,1)S(1)}, u32[]{:S(2)}, u32[]{:S(2)}) %all-to-all-start.4) | async-done | bytes 65568 | tf_op jit(solution)/shard_map/all_to_all | solution.py:32
  128.5 0.1 reshape.26
  128.7 0.2 broadcast_in_dim.10
  128.9 1.1 broadcast_in_dim.22
  130.0 4.5 %all-to-all-start.5 = ((bf16[16,8,4096]{2,1,0:T(8,128)(2,1)}), bf16[16,8,4096]{2,1,0:T(8,128)(2,1)S(1)}, u32[]{:S(2)}, u32[]{:S(2)}) async-start(bf16[16,8,4096]{2,1,0:T(8,128)(2,1)} %broadcast_in_dim.22), calls=%async_computation.5 | async-start | bytes 2097152 | tf_op jit(solution)/shard_map/all_to_all | solution.py:32
  134.6 0.2 broadcast_select_fusion.1
  134.9 2.1 %collective-permute-start.8 = (bf16[128,4096]{1,0:T(8,128)(2,1)S(1)}, bf16[128,4096]{1,0:T(8,128)(2,1)S(1)}, u32[]{:S(2)}, u32[]{:S(2)}) collective-permute-start(bf16[128,4096]{1,0:T(8,128)(2,1)S(1)} %pad_maximum_fusion.val_ref), channel_id=1, source_target_pairs={{0,64},{64,0},{1,65},{65,1},{2,66},{66,2},{3,67},{67,3},{4,68},{68... | collective-permute-start | bytes 3145736 | tf_op jit(solution)/shard_map/ppermute | solution.py:176
  137.0 11.3 %all-to-all-done.5 = bf16[16,8,4096]{2,1,0:T(8,128)(2,1)S(1)} async-done(((bf16[16,8,4096]{2,1,0:T(8,128)(2,1)}), bf16[16,8,4096]{2,1,0:T(8,128)(2,1)S(1)}, u32[]{:S(2)}, u32[]{:S(2)}) %all-to-all-start.5) | async-done | bytes 1048608 | tf_op jit(solution)/shard_map/all_to_all | solution.py:32
  148.3 4.2 %collective-permute-start = (bf16[128,4096]{1,0:T(8,128)(2,1)S(1)}, bf16[128,4096]{1,0:T(8,128)(2,1)S(1)}, u32[]{:S(2)}, u32[]{:S(2)}) collective-permute-start(bf16[128,4096]{1,0:T(8,128)(2,1)S(1)} %bitcast.16), channel_id=1, source_target_pairs={{0,64},{64,0},{1,65},{65,1},{2,66},{66,2},{3,67},{67,3},{4,68},{68... | collective-permute-start | bytes 3145736 | tf_op jit(solution)/shard_map/ppermute | solution.py:189
  152.5 2.5 %copy-done = bf16[640,4096]{1,0:T(8,128)(2,1)S(1)} copy-done((bf16[640,4096]{1,0:T(8,128)(2,1)S(1)}, bf16[640,4096]{1,0:T(8,128)(2,1)}, u32[]{:S(2)}) %copy-start) | copy-done | bytes 5242904
  155.0 2.3 %gram.2.gram_own_ref = f32[128,640]{1,0:T(8,128)S(1)} custom-call(bf16[640,4096]{1,0:T(8,128)(2,1)S(1)} %copy-done, bf16[128,4096]{1,0:T(8,128)(2,1)S(1)} %pad_maximum_fusion.val_ref), custom_call_target="tpu_custom_call" | custom-call | tf_op jit(solution)/shard_map/gram/pallas_call | solution.py:85
  157.3 2.3 %gram.3.gram_other_ref = f32[128,640]{1,0:T(8,128)S(1)} custom-call(bf16[640,4096]{1,0:T(8,128)(2,1)S(1)} %copy-done, bf16[128,4096]{1,0:T(8,128)(2,1)S(1)} %collective-permute-done.8.val_ref), custom_call_target="tpu_custom_call" | custom-call | tf_op jit(solution)/shard_map/gram/pallas_call | solution.py:85
  159.7 2.5 %copy-done.1 = bf16[640,4096]{1,0:T(8,128)(2,1)S(1)} copy-done((bf16[640,4096]{1,0:T(8,128)(2,1)S(1)}, bf16[640,4096]{1,0:T(8,128)(2,1)}, u32[]{:S(2)}) %copy-start.1) | copy-done | bytes 5242904
  162.2 2.4 %pair_values.1 = (f32[640]{0:T(1024)}, bf16[64,64]{1,0:T(8,128)(2,1)}) custom-call(bf16[640,4096]{1,0:T(8,128)(2,1)S(1)} %copy-done.1, bf16[128,4096]{1,0:T(8,128)(2,1)S(1)} %bitcast.17, bf16[128,4096]{1,0:T(8,128)(2,1)S(1)} %collective-permute-done.other_ref, f32[128,640]{1,0:T(8,128)S(1)} %gram.2.gram_own_ref, f32[128,640]{1,0:T(8,128)S(1)} %gram.3.gram_other_ref), custom_call_target="tpu_custom_call" | custom-call | tf_op jit(solution)/shard_map/pair_values/pallas_call | solution.py:117
  (25 shorter events, 0.7 us)
Async XLA Ops:
  3.4 7.5 %copy-start.2 = (bf16[64,64]{1,0:T(8,128)(2,1)S(1)}, bf16[64,64]{1,0:T(8,128)(2,1)}, u32[]{:S(2)}) copy-start(bf16[64,64]{1,0:T(8,128)(2,1)} %param.13) | copy-start | bytes 24580
  3.4 32.3 %all-to-all-start = ((bf16[8,64,1856]{2,1,0:T(8,128)(2,1)}), bf16[8,64,1856]{2,1,0:T(8,128)(2,1)S(1)}, u32[]{:S(2)}, u32[]{:S(2)}) async-start(bf16[8,64,1856]{2,1,0:T(8,128)(2,1)} %pack.1), calls=%async_computation | async-start | bytes 3932160 | tf_op jit(solution)/shard_map/all_to_all | solution.py:32
  10.9 2.9 %collective-permute-start.1 = (bf16[64,64]{1,0:T(8,128)(2,1)S(1)}, bf16[64,64]{1,0:T(8,128)(2,1)S(1)}, u32[]{:S(2)}, u32[]{:S(2)}) collective-permute-start(bf16[64,64]{1,0:T(8,128)(2,1)S(1)} %copy-done.2), channel_id=1, source_target_pairs={{0,1},{1,0},{2,3},{3,2},{4,5},{5,4},{6,7},{7,6},{8,9},{9,8},{10,11... | collective-permute-start | bytes 24584 | tf_op jit(solution)/shard_map/ppermute | solution.py:160
  13.9 4.4 %collective-permute-start.2 = (bf16[64,128]{1,0:T(8,128)(2,1)S(1)}, bf16[64,128]{1,0:T(8,128)(2,1)S(1)}, u32[]{:S(2)}, u32[]{:S(2)}) collective-permute-start(bf16[64,128]{1,0:T(8,128)(2,1)S(1)} %pad_maximum_fusion.8), channel_id=1, source_target_pairs={{0,2},{1,3},{2,0},{3,1},{4,6},{5,7},{6,4},{7,5},{8,10},{9,11},{10,... | collective-permute-start | bytes 49160 | tf_op jit(solution)/shard_map/ppermute | solution.py:160
  37.6 40.5 %all-to-all-start.1 = ((bf16[8,32,1344]{2,1,0:T(8,128)(2,1)}), bf16[8,32,1344]{2,1,0:T(8,128)(2,1)S(1)}, u32[]{:S(2)}, u32[]{:S(2)}) async-start(bf16[8,32,1344]{2,1,0:T(8,128)(2,1)} %pad_maximum_fusion.1), calls=%async_computation.1 | async-start | bytes 1441792 | tf_op jit(solution)/shard_map/all_to_all | solution.py:32
  45.8 23.6 %collective-permute-start.3 = (bf16[64,256]{1,0:T(8,128)(2,1)S(1)}, bf16[64,256]{1,0:T(8,128)(2,1)S(1)}, u32[]{:S(2)}, u32[]{:S(2)}) collective-permute-start(bf16[64,256]{1,0:T(8,128)(2,1)S(1)} %pad_maximum_fusion.7), channel_id=1, source_target_pairs={{0,4},{1,5},{2,6},{3,7},{4,0},{5,1},{6,2},{7,3},{8,12},{9,13},{10,... | collective-permute-start | bytes 98312 | tf_op jit(solution)/shard_map/ppermute | solution.py:160
  69.4 3.2 %collective-permute-start.4 = (bf16[64,512]{1,0:T(8,128)(2,1)S(1)}, bf16[64,512]{1,0:T(8,128)(2,1)S(1)}, u32[]{:S(2)}, u32[]{:S(2)}) collective-permute-start(bf16[64,512]{1,0:T(8,128)(2,1)S(1)} %pad_maximum_fusion.5), channel_id=1, source_target_pairs={{0,8},{8,0},{16,24},{24,16},{1,9},{9,1},{17,25},{25,17},{2,10},{10... | collective-permute-start | bytes 196616 | tf_op jit(solution)/shard_map/ppermute | solution.py:160
  72.6 5.4 %collective-permute-start.5 = (bf16[64,1024]{1,0:T(8,128)(2,1)S(1)}, bf16[64,1024]{1,0:T(8,128)(2,1)S(1)}, u32[]{:S(2)}, u32[]{:S(2)}) collective-permute-start(bf16[64,1024]{1,0:T(8,128)(2,1)S(1)} %pad_maximum_fusion.4), channel_id=1, source_target_pairs={{0,16},{8,24},{16,0},{24,8},{1,17},{9,25},{17,1},{25,9},{2,18},{10... | collective-permute-start | bytes 393224 | tf_op jit(solution)/shard_map/ppermute | solution.py:160
  79.2 16.4 %all-to-all-start.2 = ((bf16[8,32,896]{2,1,0:T(8,128)(2,1)}), bf16[8,32,896]{2,1,0:T(8,128)(2,1)S(1)}, u32[]{:S(2)}, u32[]{:S(2)}) async-start(bf16[8,32,896]{2,1,0:T(8,128)(2,1)} %broadcast_in_dim.8), calls=%async_computation.2 | async-start | bytes 917504 | tf_op jit(solution)/shard_map/all_to_all | solution.py:32
  82.7 6.8 %collective-permute-start.6 = (bf16[64,2048]{1,0:T(8,128)(2,1)S(1)}, bf16[64,2048]{1,0:T(8,128)(2,1)S(1)}, u32[]{:S(2)}, u32[]{:S(2)}) collective-permute-start(bf16[64,2048]{1,0:T(8,128)(2,1)S(1)} %pad_maximum_fusion.3), channel_id=1, source_target_pairs={{0,32},{32,0},{1,33},{33,1},{2,34},{34,2},{3,35},{35,3},{4,36},{36... | collective-permute-start | bytes 786440 | tf_op jit(solution)/shard_map/ppermute | solution.py:160
  96.9 20.3 %all-to-all-start.3 = ((f32[32,8,512]{2,1,0:T(8,128)}), f32[32,8,512]{2,1,0:T(8,128)S(1)}, u32[]{:S(2)}, u32[]{:S(2)}) async-start(f32[32,8,512]{2,1,0:T(8,128)} %fusion), calls=%async_computation.3 | async-start | bytes 1048576 | tf_op jit(solution)/shard_map/all_to_all | solution.py:32
  107.4 27.1 %collective-permute-start.7 = (bf16[64,4096]{1,0:T(8,128)(2,1)}, bf16[64,4096]{1,0:T(8,128)(2,1)S(1)}, u32[]{:S(2)}, u32[]{:S(2)}) collective-permute-start(bf16[64,4096]{1,0:T(8,128)(2,1)} %pad_maximum_fusion.2), channel_id=1, source_target_pairs={{0,128},{128,0},{1,129},{129,1},{2,130},{130,2},{3,131},{131,3},{4... | collective-permute-start | bytes 1572872 | tf_op jit(solution)/shard_map/ppermute | solution.py:160
  117.9 10.6 %all-to-all-start.4 = ((bf16[8,8,512]{2,1,0:T(8,128)(2,1)}), bf16[8,8,512]{2,1,0:T(8,128)(2,1)S(1)}, u32[]{:S(2)}, u32[]{:S(2)}) async-start(bf16[8,8,512]{2,1,0:T(8,128)(2,1)} %broadcast_in_dim.9), calls=%async_computation.4 | async-start | bytes 131072 | tf_op jit(solution)/shard_map/all_to_all | solution.py:32
  130.0 18.3 %all-to-all-start.5 = ((bf16[16,8,4096]{2,1,0:T(8,128)(2,1)}), bf16[16,8,4096]{2,1,0:T(8,128)(2,1)S(1)}, u32[]{:S(2)}, u32[]{:S(2)}) async-start(bf16[16,8,4096]{2,1,0:T(8,128)(2,1)} %broadcast_in_dim.22), calls=%async_computation.5 | async-start | bytes 2097152 | tf_op jit(solution)/shard_map/all_to_all | solution.py:32
  134.9 22.5 %collective-permute-start.8 = (bf16[128,4096]{1,0:T(8,128)(2,1)S(1)}, bf16[128,4096]{1,0:T(8,128)(2,1)S(1)}, u32[]{:S(2)}, u32[]{:S(2)}) collective-permute-start(bf16[128,4096]{1,0:T(8,128)(2,1)S(1)} %pad_maximum_fusion.val_ref), channel_id=1, source_target_pairs={{0,64},{64,0},{1,65},{65,1},{2,66},{66,2},{3,67},{67,3},{4,68},{68... | collective-permute-start | bytes 3145736 | tf_op jit(solution)/shard_map/ppermute | solution.py:176
  148.3 11.4 %collective-permute-start = (bf16[128,4096]{1,0:T(8,128)(2,1)S(1)}, bf16[128,4096]{1,0:T(8,128)(2,1)S(1)}, u32[]{:S(2)}, u32[]{:S(2)}) collective-permute-start(bf16[128,4096]{1,0:T(8,128)(2,1)S(1)} %bitcast.16), channel_id=1, source_target_pairs={{0,64},{64,0},{1,65},{65,1},{2,66},{66,2},{3,67},{67,3},{4,68},{68... | collective-permute-start | bytes 3145736 | tf_op jit(solution)/shard_map/ppermute | solution.py:189
  152.5 2.5 %copy-start = (bf16[640,4096]{1,0:T(8,128)(2,1)S(1)}, bf16[640,4096]{1,0:T(8,128)(2,1)}, u32[]{:S(2)}) copy-start(bf16[640,4096]{1,0:T(8,128)(2,1)} %train_ref.4) | copy-start | bytes 15728644
  159.7 2.5 %copy-start.1 = (bf16[640,4096]{1,0:T(8,128)(2,1)S(1)}, bf16[640,4096]{1,0:T(8,128)(2,1)}, u32[]{:S(2)}) copy-start(bf16[640,4096]{1,0:T(8,128)(2,1)} %train_ref.5) | copy-start | bytes 15728644

commit v4 on v3

--- a/solution.py
+++ b/solution.py
@@ -96,7 +96,7 @@
     )(train, val)
 
 
-def pair_kernel(scale, train_ref, own_ref, other_ref, gram_own_ref, gram_other_ref, out_ref, block_ref):
+def block_kernel(own_ref, block_ref):
     rows, feats = block_ref.shape
     tile = (lax.axis_index("xh") * 4 + lax.axis_index("y")) * 8 + lax.axis_index("z")
     row = pl.multiple_of(lax.axis_index("xl") * rows, rows)
@@ -104,6 +104,9 @@
     found = own_ref[pl.ds(row, rows), pl.ds(col, 2 * feats)].astype(F32)
     half = jnp.where(tile % 2 == 0, found[:, :feats], found[:, feats:])
     block_ref[...] = half.astype(BF16)
+
+
+def pair_kernel(scale, train_ref, own_ref, other_ref, gram_own_ref, gram_other_ref, out_ref):
     val = jnp.concatenate([own_ref[...], other_ref[...]], axis=0)
     grad_gram = dot_last(val, train_ref[...])
     count = own_ref.shape[0]
@@ -112,16 +115,28 @@
     out_ref[...] = total.reshape(out_ref.shape)
 
 
-def pair_values(scale, train, own, other, gram_own, gram_other, rows, feats):
-    vmem = pl.BlockSpec(memory_space=pltpu.VMEM)
+VMEM = pl.BlockSpec(memory_space=pltpu.VMEM)
+COVER = pl.CostEstimate(flops=10**10, bytes_accessed=32 * 2**20, transcendentals=0)
+
+
+def own_block(own, rows, feats):
+    return pl.pallas_call(
+        block_kernel,
+        out_shape=jax.ShapeDtypeStruct((rows, feats), BF16),
+        in_specs=[VMEM],
+        out_specs=VMEM,
+        compiler_params=pltpu.CompilerParams(vmem_limit_bytes=8 * 1024 * 1024),
+        cost_estimate=COVER,
+        name="own_block",
+    )(own)
+
+
+def pair_values(scale, train, own, other, gram_own, gram_other):
     return pl.pallas_call(
         functools.partial(pair_kernel, scale),
-        out_shape=(
-            jax.ShapeDtypeStruct((train.shape[0],), F32),
-            jax.ShapeDtypeStruct((rows, feats), BF16),
-        ),
-        in_specs=[vmem] * 5,
-        out_specs=(vmem, vmem),
+        out_shape=jax.ShapeDtypeStruct((train.shape[0],), F32),
+        in_specs=[VMEM] * 5,
+        out_specs=VMEM,
         compiler_params=pltpu.CompilerParams(vmem_limit_bytes=24 * 1024 * 1024),
         name="pair_values",
     )(train, own, other, gram_own, gram_other)
@@ -187,10 +202,9 @@
     val_z = val_z.transpose(1, 2, 0, 3).reshape(chunk, width)
     val_own = share(val_z, CHIPS, n_chips).reshape(n_chips * chunk, width)
     val_other = lax.ppermute(val_own, "c", swap)
+    block = own_block(val_own, attn_rows, feats)
     scale = 1.0 / (width * math.sqrt(vals))
-    influence, block = pair_values(
-        scale, train_grads, val_own, val_other, gram_own, gram_other, attn_rows, feats
-    )
+    influence = pair_values(scale, train_grads, val_own, val_other, gram_own, gram_other)
     return (influence, block)
 
 

time: 165 us -> 164 us (level)
  local copies, waits for them, and re-layouts: 8.29 us -> 6.27 us
    all_to_all x6, waiting for transfers between devices: 50 us -> 45.6 us  [trade(): return lax.all_to_all(value, axes, 0, 0, tiled=True)]
    ppermute x7, waiting for transfers between devices: 33.1 us -> 37.6 us  [local(): theirs = lax.ppermute(attn, axis, pairs)]
    unnamed x8 -> x10, local copies, waits for them, and re-layouts: 5.06 us -> 3.11 us
  transfers between devices with their start and end apart: 15 -> 15, of which waited for: 11 -> 12; matrix products, arithmetic and copies ran while one was open for 2% -> 2% of each run, Pallas kernels for 3% -> 3%
where the time goes in v4:
time: 164 us; the launch traced here: 163 us
  waiting for transfers between devices  83.1 us (51%)
  starting transfers between devices  57.5 us (35%)
  Pallas kernels  10.5 us (6%)
  local copies, waits for them, and re-layouts  6.27 us (4%)
  other arithmetic  3 us (2%)
  matrix products  2.09 us (1%)
    all_to_all x6, waiting for transfers between devices, trade(): return lax.all_to_all(value, axes, 0, 0, tiled=True)  45.6 us
    ppermute x7, waiting for transfers between devices, local(): theirs = lax.ppermute(attn, axis, pairs)  37.6 us
    all_to_all x6, starting transfers between devices, trade(): return lax.all_to_all(value, axes, 0, 0, tiled=True)  36.9 us
    ppermute x7, starting transfers between devices, local(): theirs = lax.ppermute(attn, axis, pairs)  14.6 us
    pallas_call x2, Pallas kernels, gram(): pl.pallas_call(gram_kernel, grid=(tokens // block,), in_specs=[pl.BlockSp...  4.62 us
    ppermute x1, starting transfers between devices, local(): val_other = lax.ppermute(val_own, 'c', swap)  4.05 us
  transfers between devices with their start and end apart: 15, of which 12 were waited for; matrix products, arithmetic and copies ran while one was open for 2% of the time, Pallas kernels for 3%

profile of v4, /device:TPU:1, one launch (start us, length us, event | category | flops | bytes accessed | tf_op | source)
XLA Modules:
  0.0 163.4 jit_solution(15079580553786026178)
XLA Ops:
  0.6 2.8 %pack.1 = bf16[8,64,1856]{2,1,0:T(8,128)(2,1)} custom-call(bf16[64,256]{1,0:T(8,128)(2,1)} %bitcast.31, bf16[64,256]{1,0:T(8,128)(2,1)} %bitcast.32, bf16[64,3584]{1,0:T(8,128)(2,1)} %gate_ref.1, bf16[64,3584]{1,0:T(8,128)(2,1)} %up_ref.1, bf16[64,3584]{1,0:T(8,128)(2,1)} %bitcast.29), custom_call_target="tpu_custom_call" | custom-call | tf_op jit(solution)/shard_map/pack/pallas_call | solution.py:68
  3.4 7.5 %all-to-all-start = ((bf16[8,64,1856]{2,1,0:T(8,128)(2,1)}), bf16[8,64,1856]{2,1,0:T(8,128)(2,1)S(1)}, u32[]{:S(2)}, u32[]{:S(2)}) async-start(bf16[8,64,1856]{2,1,0:T(8,128)(2,1)} %pack.1), calls=%async_computation | async-start | bytes 3932160 | tf_op jit(solution)/shard_map/all_to_all | solution.py:32
  10.9 1.7 %collective-permute-start.1 = (bf16[64,64]{1,0:T(8,128)(2,1)S(1)}, bf16[64,64]{1,0:T(8,128)(2,1)S(1)}, u32[]{:S(2)}, u32[]{:S(2)}) collective-permute-start(bf16[64,64]{1,0:T(8,128)(2,1)S(1)} %copy-done.1), channel_id=1, source_target_pairs={{0,1},{1,0},{2,3},{3,2},{4,5},{5,4},{6,7},{7,6},{8,9},{9,8},{10,11... | collective-permute-start | bytes 24584 | tf_op jit(solution)/shard_map/ppermute | solution.py:175
  12.6 1.1 collective-permute-done.1
  13.9 3.0 %collective-permute-start.2 = (bf16[64,128]{1,0:T(8,128)(2,1)S(1)}, bf16[64,128]{1,0:T(8,128)(2,1)S(1)}, u32[]{:S(2)}, u32[]{:S(2)}) collective-permute-start(bf16[64,128]{1,0:T(8,128)(2,1)S(1)} %pad_maximum_fusion.8), channel_id=1, source_target_pairs={{0,2},{1,3},{2,0},{3,1},{4,6},{5,7},{6,4},{7,5},{8,10},{9,11},{10,... | collective-permute-start | bytes 49160 | tf_op jit(solution)/shard_map/ppermute | solution.py:175
  16.9 1.4 collective-permute-done.2
  18.4 17.3 %all-to-all-done = bf16[8,64,1856]{2,1,0:T(8,128)(2,1)S(1)} async-done(((bf16[8,64,1856]{2,1,0:T(8,128)(2,1)}), bf16[8,64,1856]{2,1,0:T(8,128)(2,1)S(1)}, u32[]{:S(2)}, u32[]{:S(2)}) %all-to-all-start) | async-done | bytes 1900576 | tf_op jit(solution)/shard_map/all_to_all | solution.py:32
  35.7 0.3 convolution_convert_fusion.1
  36.0 0.5 convolution_convert_fusion
  36.5 0.1 copy.21
  36.7 0.9 pad_maximum_fusion.1
  37.6 8.2 %all-to-all-start.1 = ((bf16[8,32,1344]{2,1,0:T(8,128)(2,1)}), bf16[8,32,1344]{2,1,0:T(8,128)(2,1)S(1)}, u32[]{:S(2)}, u32[]{:S(2)}) async-start(bf16[8,32,1344]{2,1,0:T(8,128)(2,1)} %pad_maximum_fusion.1), calls=%async_computation.1 | async-start | bytes 1441792 | tf_op jit(solution)/shard_map/all_to_all | solution.py:32
  45.8 5.5 %collective-permute-start.3 = (bf16[64,256]{1,0:T(8,128)(2,1)S(1)}, bf16[64,256]{1,0:T(8,128)(2,1)S(1)}, u32[]{:S(2)}, u32[]{:S(2)}) collective-permute-start(bf16[64,256]{1,0:T(8,128)(2,1)S(1)} %pad_maximum_fusion.7), channel_id=1, source_target_pairs={{0,4},{1,5},{2,6},{3,7},{4,0},{5,1},{6,2},{7,3},{8,12},{9,13},{10,... | collective-permute-start | bytes 98312 | tf_op jit(solution)/shard_map/ppermute | solution.py:175
  51.2 18.1 %collective-permute-done.3 = bf16[64,256]{1,0:T(8,128)(2,1)S(1)} collective-permute-done((bf16[64,256]{1,0:T(8,128)(2,1)S(1)}, bf16[64,256]{1,0:T(8,128)(2,1)S(1)}, u32[]{:S(2)}, u32[]{:S(2)}) %collective-permute-start.3) | collective-permute-done | bytes 32800 | tf_op jit(solution)/shard_map/ppermute | solution.py:175
  69.4 0.1 collective-permute-start.4
  69.5 3.1 %collective-permute-done.4 = bf16[64,512]{1,0:T(8,128)(2,1)S(1)} collective-permute-done((bf16[64,512]{1,0:T(8,128)(2,1)S(1)}, bf16[64,512]{1,0:T(8,128)(2,1)S(1)}, u32[]{:S(2)}, u32[]{:S(2)}) %collective-permute-start.4) | collective-permute-done | bytes 65568 | tf_op jit(solution)/shard_map/ppermute | solution.py:175
  72.6 0.1 collective-permute-start.5
  72.7 5.3 %collective-permute-done.5 = bf16[64,1024]{1,0:T(8,128)(2,1)S(1)} collective-permute-done((bf16[64,1024]{1,0:T(8,128)(2,1)S(1)}, bf16[64,1024]{1,0:T(8,128)(2,1)S(1)}, u32[]{:S(2)}, u32[]{:S(2)}) %collective-permute-start.5) | collective-permute-done | bytes 131104 | tf_op jit(solution)/shard_map/ppermute | solution.py:175
  78.1 0.1 convert_reduce_fusion
  78.4 0.8 broadcast_in_dim.8
  79.2 3.5 %all-to-all-start.2 = ((bf16[8,32,896]{2,1,0:T(8,128)(2,1)}), bf16[8,32,896]{2,1,0:T(8,128)(2,1)S(1)}, u32[]{:S(2)}, u32[]{:S(2)}) async-start(bf16[8,32,896]{2,1,0:T(8,128)(2,1)} %broadcast_in_dim.8), calls=%async_computation.2 | async-start | bytes 917504 | tf_op jit(solution)/shard_map/all_to_all | solution.py:32
  82.7 2.8 %collective-permute-start.6 = (bf16[64,2048]{1,0:T(8,128)(2,1)S(1)}, bf16[64,2048]{1,0:T(8,128)(2,1)S(1)}, u32[]{:S(2)}, u32[]{:S(2)}) collective-permute-start(bf16[64,2048]{1,0:T(8,128)(2,1)S(1)} %pad_maximum_fusion.3), channel_id=1, source_target_pairs={{0,32},{32,0},{1,33},{33,1},{2,34},{34,2},{3,35},{35,3},{4,36},{36... | collective-permute-start | bytes 786440 | tf_op jit(solution)/shard_map/ppermute | solution.py:175
  85.5 4.0 %collective-permute-done.6 = bf16[64,2048]{1,0:T(8,128)(2,1)S(1)} collective-permute-done((bf16[64,2048]{1,0:T(8,128)(2,1)S(1)}, bf16[64,2048]{1,0:T(8,128)(2,1)S(1)}, u32[]{:S(2)}, u32[]{:S(2)}) %collective-permute-start.6) | collective-permute-done | bytes 262176 | tf_op jit(solution)/shard_map/ppermute | solution.py:175
  89.5 0.1 broadcast_select_fusion.3
  89.6 6.0 %all-to-all-done.2 = bf16[8,32,896]{2,1,0:T(8,128)(2,1)S(1)} async-done(((bf16[8,32,896]{2,1,0:T(8,128)(2,1)}), bf16[8,32,896]{2,1,0:T(8,128)(2,1)S(1)}, u32[]{:S(2)}, u32[]{:S(2)}) %all-to-all-start.2) | async-done | bytes 458784 | tf_op jit(solution)/shard_map/all_to_all | solution.py:32
  95.6 1.3 fusion
  96.9 9.7 %all-to-all-start.3 = ((f32[32,8,512]{2,1,0:T(8,128)}), f32[32,8,512]{2,1,0:T(8,128)S(1)}, u32[]{:S(2)}, u32[]{:S(2)}) async-start(f32[32,8,512]{2,1,0:T(8,128)} %fusion), calls=%async_computation.3 | async-start | bytes 1048576 | tf_op jit(solution)/shard_map/all_to_all | solution.py:32
  106.6 1.5 collective-permute-start.7
  108.1 0.1 constant_dynamic-slice_fusion
  108.3 8.9 %all-to-all-done.3 = f32[32,8,512]{2,1,0:T(8,128)S(1)} async-done(((f32[32,8,512]{2,1,0:T(8,128)}), f32[32,8,512]{2,1,0:T(8,128)S(1)}, u32[]{:S(2)}, u32[]{:S(2)}) %all-to-all-start.3) | async-done | bytes 524320 | tf_op jit(solution)/shard_map/all_to_all | solution.py:32
  117.2 0.6 broadcast_in_dim.9
  117.9 3.3 %all-to-all-start.4 = ((bf16[8,8,512]{2,1,0:T(8,128)(2,1)}), bf16[8,8,512]{2,1,0:T(8,128)(2,1)S(1)}, u32[]{:S(2)}, u32[]{:S(2)}) async-start(bf16[8,8,512]{2,1,0:T(8,128)(2,1)} %broadcast_in_dim.9), calls=%async_computation.4 | async-start | bytes 131072 | tf_op jit(solution)/shard_map/all_to_all | solution.py:32
  121.2 4.5 %collective-permute-done.7 = bf16[64,4096]{1,0:T(8,128)(2,1)} collective-permute-done((bf16[64,4096]{1,0:T(8,128)(2,1)S(1)}, bf16[64,4096]{1,0:T(8,128)(2,1)}, u32[]{:S(2)}, u32[]{:S(2)}) %collective-permute-start.7) | collective-permute-done | bytes 524320 | tf_op jit(solution)/shard_map/ppermute | solution.py:175
  125.7 1.2 broadcast_select_fusion.1
  126.9 1.5 all-to-all-done.4
  128.5 0.1 reshape.26
  128.7 0.2 broadcast_in_dim.10
  128.9 1.1 broadcast_in_dim.22
  130.0 4.7 %all-to-all-start.5 = ((bf16[16,8,4096]{2,1,0:T(8,128)(2,1)}), bf16[16,8,4096]{2,1,0:T(8,128)(2,1)S(1)}, u32[]{:S(2)}, u32[]{:S(2)}) async-start(bf16[16,8,4096]{2,1,0:T(8,128)(2,1)} %broadcast_in_dim.22), calls=%async_computation.5 | async-start | bytes 2097152 | tf_op jit(solution)/shard_map/all_to_all | solution.py:32
  134.8 1.9 %collective-permute-start.8 = (bf16[128,4096]{1,0:T(8,128)(2,1)S(1)}, bf16[128,4096]{1,0:T(8,128)(2,1)S(1)}, u32[]{:S(2)}, u32[]{:S(2)}) collective-permute-start(bf16[128,4096]{1,0:T(8,128)(2,1)S(1)} %pad_maximum_fusion.val_ref), channel_id=1, source_target_pairs={{0,64},{64,0},{1,65},{65,1},{2,66},{66,2},{3,67},{67,3},{4,68},{68... | collective-permute-start | bytes 3145736 | tf_op jit(solution)/shard_map/ppermute | solution.py:191
  136.7 11.8 %all-to-all-done.5 = bf16[16,8,4096]{2,1,0:T(8,128)(2,1)S(1)} async-done(((bf16[16,8,4096]{2,1,0:T(8,128)(2,1)}), bf16[16,8,4096]{2,1,0:T(8,128)(2,1)S(1)}, u32[]{:S(2)}, u32[]{:S(2)}) %all-to-all-start.5) | async-done | bytes 1048608 | tf_op jit(solution)/shard_map/all_to_all | solution.py:32
  148.5 4.1 %collective-permute-start = (bf16[128,4096]{1,0:T(8,128)(2,1)S(1)}, bf16[128,4096]{1,0:T(8,128)(2,1)S(1)}, u32[]{:S(2)}, u32[]{:S(2)}) collective-permute-start(bf16[128,4096]{1,0:T(8,128)(2,1)S(1)} %bitcast.18), channel_id=1, source_target_pairs={{0,64},{64,0},{1,65},{65,1},{2,66},{66,2},{3,67},{67,3},{4,68},{68... | collective-permute-start | bytes 3145736 | tf_op jit(solution)/shard_map/ppermute | solution.py:204
  152.6 2.5 %copy-done = bf16[640,4096]{1,0:T(8,128)(2,1)S(1)} copy-done((bf16[640,4096]{1,0:T(8,128)(2,1)S(1)}, bf16[640,4096]{1,0:T(8,128)(2,1)}, u32[]{:S(2)}) %copy-start) | copy-done | bytes 5242904
  155.1 2.3 %gram.2.gram_own_ref = f32[128,640]{1,0:T(8,128)S(1)} custom-call(bf16[640,4096]{1,0:T(8,128)(2,1)S(1)} %copy-done, bf16[128,4096]{1,0:T(8,128)(2,1)S(1)} %pad_maximum_fusion.val_ref), custom_call_target="tpu_custom_call" | custom-call | tf_op jit(solution)/shard_map/gram/pallas_call | solution.py:85
  157.4 2.3 %gram.3.gram_other_ref = f32[128,640]{1,0:T(8,128)S(1)} custom-call(bf16[640,4096]{1,0:T(8,128)(2,1)S(1)} %copy-done, bf16[128,4096]{1,0:T(8,128)(2,1)S(1)} %collective-permute-done.8.val_ref), custom_call_target="tpu_custom_call" | custom-call | tf_op jit(solution)/shard_map/gram/pallas_call | solution.py:85
  159.8 0.7 own_block.1
  160.5 0.5 slice-done.1
  161.0 2.4 %pair_values.1 = f32[640]{0:T(1024)} custom-call(bf16[640,4096]{1,0:T(8,128)(2,1)S(1)} %bitcast.17, bf16[128,4096]{1,0:T(8,128)(2,1)S(1)} %bitcast.20, bf16[128,4096]{1,0:T(8,128)(2,1)S(1)} %collective-permute-done.other_ref, f32[128,640]{1,0:T(8,128)S(1)} %gram.2.gram_own_ref, f32[128,640]{1,0:T(8,128)S(1)} %gram.3.gram_other_ref), custom_call_target="tpu_custom_call" | custom-call | tf_op jit(solution)/shard_map/pair_values/pallas_call | solution.py:135
  (29 shorter events, 0.9 us)
Async XLA Ops:
  3.4 7.5 %copy-start.1 = (bf16[64,64]{1,0:T(8,128)(2,1)S(1)}, bf16[64,64]{1,0:T(8,128)(2,1)}, u32[]{:S(2)}) copy-start(bf16[64,64]{1,0:T(8,128)(2,1)} %param.13) | copy-start | bytes 24580
  3.4 32.3 %all-to-all-start = ((bf16[8,64,1856]{2,1,0:T(8,128)(2,1)}), bf16[8,64,1856]{2,1,0:T(8,128)(2,1)S(1)}, u32[]{:S(2)}, u32[]{:S(2)}) async-start(bf16[8,64,1856]{2,1,0:T(8,128)(2,1)} %pack.1), calls=%async_computation | async-start | bytes 3932160 | tf_op jit(solution)/shard_map/all_to_all | solution.py:32
  10.9 2.9 %collective-permute-start.1 = (bf16[64,64]{1,0:T(8,128)(2,1)S(1)}, bf16[64,64]{1,0:T(8,128)(2,1)S(1)}, u32[]{:S(2)}, u32[]{:S(2)}) collective-permute-start(bf16[64,64]{1,0:T(8,128)(2,1)S(1)} %copy-done.1), channel_id=1, source_target_pairs={{0,1},{1,0},{2,3},{3,2},{4,5},{5,4},{6,7},{7,6},{8,9},{9,8},{10,11... | collective-permute-start | bytes 24584 | tf_op jit(solution)/shard_map/ppermute | solution.py:175
  13.9 4.4 %collective-permute-start.2 = (bf16[64,128]{1,0:T(8,128)(2,1)S(1)}, bf16[64,128]{1,0:T(8,128)(2,1)S(1)}, u32[]{:S(2)}, u32[]{:S(2)}) collective-permute-start(bf16[64,128]{1,0:T(8,128)(2,1)S(1)} %pad_maximum_fusion.8), channel_id=1, source_target_pairs={{0,2},{1,3},{2,0},{3,1},{4,6},{5,7},{6,4},{7,5},{8,10},{9,11},{10,... | collective-permute-start | bytes 49160 | tf_op jit(solution)/shard_map/ppermute | solution.py:175
  37.6 40.5 %all-to-all-start.1 = ((bf16[8,32,1344]{2,1,0:T(8,128)(2,1)}), bf16[8,32,1344]{2,1,0:T(8,128)(2,1)S(1)}, u32[]{:S(2)}, u32[]{:S(2)}) async-start(bf16[8,32,1344]{2,1,0:T(8,128)(2,1)} %pad_maximum_fusion.1), calls=%async_computation.1 | async-start | bytes 1441792 | tf_op jit(solution)/shard_map/all_to_all | solution.py:32
  45.8 23.6 %collective-permute-start.3 = (bf16[64,256]{1,0:T(8,128)(2,1)S(1)}, bf16[64,256]{1,0:T(8,128)(2,1)S(1)}, u32[]{:S(2)}, u32[]{:S(2)}) collective-permute-start(bf16[64,256]{1,0:T(8,128)(2,1)S(1)} %pad_maximum_fusion.7), channel_id=1, source_target_pairs={{0,4},{1,5},{2,6},{3,7},{4,0},{5,1},{6,2},{7,3},{8,12},{9,13},{10,... | collective-permute-start | bytes 98312 | tf_op jit(solution)/shard_map/ppermute | solution.py:175
  69.4 3.2 %collective-permute-start.4 = (bf16[64,512]{1,0:T(8,128)(2,1)S(1)}, bf16[64,512]{1,0:T(8,128)(2,1)S(1)}, u32[]{:S(2)}, u32[]{:S(2)}) collective-permute-start(bf16[64,512]{1,0:T(8,128)(2,1)S(1)} %pad_maximum_fusion.5), channel_id=1, source_target_pairs={{0,8},{8,0},{16,24},{24,16},{1,9},{9,1},{17,25},{25,17},{2,10},{10... | collective-permute-start | bytes 196616 | tf_op jit(solution)/shard_map/ppermute | solution.py:175
  72.6 5.4 %collective-permute-start.5 = (bf16[64,1024]{1,0:T(8,128)(2,1)S(1)}, bf16[64,1024]{1,0:T(8,128)(2,1)S(1)}, u32[]{:S(2)}, u32[]{:S(2)}) collective-permute-start(bf16[64,1024]{1,0:T(8,128)(2,1)S(1)} %pad_maximum_fusion.4), channel_id=1, source_target_pairs={{0,16},{8,24},{16,0},{24,8},{1,17},{9,25},{17,1},{25,9},{2,18},{10... | collective-permute-start | bytes 393224 | tf_op jit(solution)/shard_map/ppermute | solution.py:175
  79.2 16.4 %all-to-all-start.2 = ((bf16[8,32,896]{2,1,0:T(8,128)(2,1)}), bf16[8,32,896]{2,1,0:T(8,128)(2,1)S(1)}, u32[]{:S(2)}, u32[]{:S(2)}) async-start(bf16[8,32,896]{2,1,0:T(8,128)(2,1)} %broadcast_in_dim.8), calls=%async_computation.2 | async-start | bytes 917504 | tf_op jit(solution)/shard_map/all_to_all | solution.py:32
  82.7 6.8 %collective-permute-start.6 = (bf16[64,2048]{1,0:T(8,128)(2,1)S(1)}, bf16[64,2048]{1,0:T(8,128)(2,1)S(1)}, u32[]{:S(2)}, u32[]{:S(2)}) collective-permute-start(bf16[64,2048]{1,0:T(8,128)(2,1)S(1)} %pad_maximum_fusion.3), channel_id=1, source_target_pairs={{0,32},{32,0},{1,33},{33,1},{2,34},{34,2},{3,35},{35,3},{4,36},{36... | collective-permute-start | bytes 786440 | tf_op jit(solution)/shard_map/ppermute | solution.py:175
  96.9 20.3 %all-to-all-start.3 = ((f32[32,8,512]{2,1,0:T(8,128)}), f32[32,8,512]{2,1,0:T(8,128)S(1)}, u32[]{:S(2)}, u32[]{:S(2)}) async-start(f32[32,8,512]{2,1,0:T(8,128)} %fusion), calls=%async_computation.3 | async-start | bytes 1048576 | tf_op jit(solution)/shard_map/all_to_all | solution.py:32
  106.6 19.1 %collective-permute-start.7 = (bf16[64,4096]{1,0:T(8,128)(2,1)S(1)}, bf16[64,4096]{1,0:T(8,128)(2,1)}, u32[]{:S(2)}, u32[]{:S(2)}) collective-permute-start(bf16[64,4096]{1,0:T(8,128)(2,1)S(1)} %pad_maximum_fusion.2), channel_id=1, source_target_pairs={{0,128},{128,0},{1,129},{129,1},{2,130},{130,2},{3,131},{131,3},{4... | collective-permute-start | bytes 1572872 | tf_op jit(solution)/shard_map/ppermute | solution.py:175
  117.9 10.6 %all-to-all-start.4 = ((bf16[8,8,512]{2,1,0:T(8,128)(2,1)}), bf16[8,8,512]{2,1,0:T(8,128)(2,1)S(1)}, u32[]{:S(2)}, u32[]{:S(2)}) async-start(bf16[8,8,512]{2,1,0:T(8,128)(2,1)} %broadcast_in_dim.9), calls=%async_computation.4 | async-start | bytes 131072 | tf_op jit(solution)/shard_map/all_to_all | solution.py:32
  130.0 18.6 %all-to-all-start.5 = ((bf16[16,8,4096]{2,1,0:T(8,128)(2,1)}), bf16[16,8,4096]{2,1,0:T(8,128)(2,1)S(1)}, u32[]{:S(2)}, u32[]{:S(2)}) async-start(bf16[16,8,4096]{2,1,0:T(8,128)(2,1)} %broadcast_in_dim.22), calls=%async_computation.5 | async-start | bytes 2097152 | tf_op jit(solution)/shard_map/all_to_all | solution.py:32
  134.8 22.6 %collective-permute-start.8 = (bf16[128,4096]{1,0:T(8,128)(2,1)S(1)}, bf16[128,4096]{1,0:T(8,128)(2,1)S(1)}, u32[]{:S(2)}, u32[]{:S(2)}) collective-permute-start(bf16[128,4096]{1,0:T(8,128)(2,1)S(1)} %pad_maximum_fusion.val_ref), channel_id=1, source_target_pairs={{0,64},{64,0},{1,65},{65,1},{2,66},{66,2},{3,67},{67,3},{4,68},{68... | collective-permute-start | bytes 3145736 | tf_op jit(solution)/shard_map/ppermute | solution.py:191
  148.5 11.9 %collective-permute-start = (bf16[128,4096]{1,0:T(8,128)(2,1)S(1)}, bf16[128,4096]{1,0:T(8,128)(2,1)S(1)}, u32[]{:S(2)}, u32[]{:S(2)}) collective-permute-start(bf16[128,4096]{1,0:T(8,128)(2,1)S(1)} %bitcast.18), channel_id=1, source_target_pairs={{0,64},{64,0},{1,65},{65,1},{2,66},{66,2},{3,67},{67,3},{4,68},{68... | collective-permute-start | bytes 3145736 | tf_op jit(solution)/shard_map/ppermute | solution.py:204
  152.6 2.5 %copy-start = (bf16[640,4096]{1,0:T(8,128)(2,1)S(1)}, bf16[640,4096]{1,0:T(8,128)(2,1)}, u32[]{:S(2)}) copy-start(bf16[640,4096]{1,0:T(8,128)(2,1)} %train_ref.4) | copy-start | bytes 15728644
  157.4 3.1 %slice-start = ((s8[5242880]{0:T(1024)(128)(4,1)}), s8[4194304]{0:T(1024)(128)(4,1)S(1)}, s32[]{:S(2)}) async-start(s8[5242880]{0:T(1024)(128)(4,1)} %bitcast.16), calls=%async_computation.6 | async-start | bytes 8388608
  159.7 1.2 slice-start.1

commit v5 on v4

--- a/solution.py
+++ b/solution.py
@@ -44,19 +44,41 @@
     return lax.dot_general(left, right, (((1,), (1,)), ((), ())), preferred_element_type=F32)
 
 
-def pack_kernel(in_ref, grad_ref, gate_ref, up_ref, down_ref, out_ref, held, sems):
+def pack_kernel(in_hbm, grad_hbm, gate_hbm, up_hbm, down_hbm, out_ref, *scratch):
+    in_ref, grad_ref, gate_ref, up_ref, down_ref, held, in_sems, out_sems = scratch
     vals = in_ref.shape[1]
+    peers = out_ref.shape[0]
     own = (out_ref.shape[2] - 2 * vals) // 3
+    groups = peers // 2
+    small = [
+        pltpu.make_async_copy(in_hbm, in_ref, in_sems.at[3 * groups]),
+        pltpu.make_async_copy(grad_hbm, grad_ref, in_sems.at[3 * groups + 1]),
+    ]
+    for copy in small:
+        copy.start()
+    loads = []
+    sides = ((gate_hbm, gate_ref), (up_hbm, up_ref), (down_hbm, down_ref))
+    for group in range(groups):
+        here = pl.ds(group * 2 * own, 2 * own)
+        for i, (source, target) in enumerate(sides):
+            sem = in_sems.at[3 * group + i]
+            loads.append(pltpu.make_async_copy(source.at[:, here], target.at[:, here], sem))
+            loads[-1].start()
+    for copy in small:
+        copy.wait()
     copies = []
-    for peer in range(out_ref.shape[0]):
+    for peer in range(peers):
+        if peer % 2 == 0:
+            for i in range(3):
+                loads[3 * (peer // 2) + i].wait()
         here = slice(peer * own, (peer + 1) * own)
         held[peer, :, :vals] = in_ref[...]
         held[peer, :, vals : 2 * vals] = grad_ref[...]
         start = 2 * vals
-        for ref in (gate_ref, up_ref, down_ref):
+        for _, ref in sides:
             held[peer, :, start : start + own] = ref[:, here]
             start += own
-        copies.append(pltpu.make_async_copy(held.at[peer], out_ref.at[peer], sems.at[peer]))
+        copies.append(pltpu.make_async_copy(held.at[peer], out_ref.at[peer], out_sems.at[peer]))
         copies[-1].start()
     for copy in copies:
         copy.wait()
@@ -65,13 +87,67 @@
 def pack(inputs_t, out_grad_t, w_gate, w_up, w_down_t, peers):
     feats, vals = inputs_t.shape
     shape = (peers, feats, 2 * vals + 3 * (w_gate.shape[1] // peers))
+    arrays = (inputs_t, out_grad_t, w_gate, w_up, w_down_t)
     return pl.pallas_call(
         pack_kernel,
+        in_specs=[pl.BlockSpec(memory_space=pl.ANY)] * 5,
         out_specs=pl.BlockSpec(memory_space=pl.ANY),
         out_shape=jax.ShapeDtypeStruct(shape, BF16),
-        scratch_shapes=[pltpu.VMEM(shape, BF16), pltpu.SemaphoreType.DMA((peers,))],
+        scratch_shapes=[pltpu.VMEM(value.shape, BF16) for value in arrays]
+        + [
+            pltpu.VMEM(shape, BF16),
+            pltpu.SemaphoreType.DMA((3 * (peers // 2) + 2,)),
+            pltpu.SemaphoreType.DMA((peers,)),
+        ],
         name="pack",
-    )(inputs_t, out_grad_t, w_gate, w_up, w_down_t)
+    )(*arrays)
+
+
+def fan_kernel(got_ref, out_ref, held, sems):
+    n_z, _, wide = got_ref.shape
+    feats = 64
+    for place in range(wide // feats):
+        here = slice(place * feats, (place + 1) * feats)
+        for z in range(0, n_z, 2):
+            start = (place * n_z + z) * feats
+            pair = jnp.concatenate([got_ref[z, :, here], got_ref[z + 1, :, here]], axis=1)
+            held[:, start : start + 2 * feats] = pair
+    copies = [
+        pltpu.make_async_copy(held, out_ref.at[i], sems.at[i]) for i in range(out_ref.shape[0])
+    ]
+    for copy in copies:
+        copy.start()
+    for copy in copies:
+        copy.wait()
+
+
+def fan_out(got, count):
+    n_z, rows, wide = got.shape
+    return pl.pallas_call(
+        fan_kernel,
+        in_specs=[pl.BlockSpec(memory_space=pltpu.VMEM)],
+        out_specs=pl.BlockSpec(memory_space=pl.ANY),
+        out_shape=jax.ShapeDtypeStruct((count, rows, n_z * wide), BF16),
+        scratch_shapes=[pltpu.VMEM((rows, n_z * wide), BF16), pltpu.SemaphoreType.DMA((count,))],
+        compiler_params=pltpu.CompilerParams(vmem_limit_bytes=4 * 1024 * 1024),
+        name="fan_out",
+    )(got)
+
+
+def backward_kernel(first, grads_ref, got_ref, out_ref):
+    weights = got_ref[:, first : first + grads_ref.shape[1]]
+    out_ref[...] = dot_last(grads_ref[...], weights).astype(out_ref.dtype)
+
+
+def backward(first, grads, got):
+    vmem = pl.BlockSpec(memory_space=pltpu.VMEM)
+    return pl.pallas_call(
+        functools.partial(backward_kernel, first),
+        out_shape=jax.ShapeDtypeStruct((grads.shape[0], got.shape[0]), BF16),
+        in_specs=[vmem] * 2,
+        compiler_params=pltpu.CompilerParams(vmem_limit_bytes=8 * 1024 * 1024),
+        name="backward",
+    )(grads, got)
 
 
 def gram_kernel(train_ref, val_ref, out_ref):
@@ -189,18 +265,18 @@
     grads = act_grads(pre[:, :own], pre[:, own : 2 * own], pre[:, 2 * own :])
     grads = share(grads, "z", n_z).reshape(vals, 2 * own)
     attn_other = lax.ppermute(attn, "c", swap)
-    part = dot_last(grads, back_w)
+    part = backward(first_w, grads, got)
     parts = trade(part.reshape(n_hidplane, chunk, wide), HIDPLANE)
 
     gram_own = gram(train_inputs, attn)
     gram_other = gram(train_inputs, attn_other)
-    dx = jnp.sum(parts, axis=0)
+    dx = jnp.sum(parts.astype(F32), axis=0)
     mine = lax.dynamic_slice_in_dim(got[:, vals:first_w], row, chunk, 1).T
     mine = lax.optimization_barrier(mine)
     val_grad = (mine.astype(F32) + dx).astype(BF16)
-    val_z = share(val_grad, "z", n_z).reshape(n_z, chunk, n_plane, feats)
-    val_z = val_z.transpose(1, 2, 0, 3).reshape(chunk, width)
-    val_own = share(val_z, CHIPS, n_chips).reshape(n_chips * chunk, width)
+    val_z = share(val_grad, "z", n_z)
+    sent = fan_out(val_z, n_chips)
+    val_own = trade(sent, CHIPS).reshape(n_chips * chunk, width)
     val_other = lax.ppermute(val_own, "c", swap)
     block = own_block(val_own, attn_rows, feats)
     scale = 1.0 / (width * math.sqrt(vals))

time: 164 us -> 161 us (0.982)
  Pallas kernels: 10.5 us -> 12.8 us
  waiting for transfers between devices: 83.1 us -> 80.9 us
    pallas_call x1 -> x3, Pallas kernels: 2.77 us -> 5.03 us  [the longest x1 2.61 us: pack(): pl.pallas_call(pack_kernel, in_specs=[pl.BlockSpec(memory_space=pl.ANY)]...]
where the time goes in v5:
time: 161 us
  waiting for transfers between devices  80.9 us (50%)
  starting transfers between devices  56.7 us (35%)
  Pallas kernels  12.8 us (8%)
  local copies, waits for them, and re-layouts  4.79 us (3%)
  other arithmetic  3.83 us (2%)
    all_to_all x6, waiting for transfers between devices, trade(): return lax.all_to_all(value, axes, 0, 0, tiled=True)  44 us
    all_to_all x6, starting transfers between devices, trade(): return lax.all_to_all(value, axes, 0, 0, tiled=True)  37.2 us
    ppermute x7, waiting for transfers between devices, local(): theirs = lax.ppermute(attn, axis, pairs)  36.9 us
    ppermute x7, starting transfers between devices, local(): theirs = lax.ppermute(attn, axis, pairs)  14.6 us
    pallas_call x2, Pallas kernels, gram(): pl.pallas_call(gram_kernel, grid=(tokens // block,), in_specs=[pl.BlockSp...  4.61 us
    ppermute x1, starting transfers between devices, local(): val_other = lax.ppermute(val_own, 'c', swap)  3.43 us
  transfers between devices with their start and end apart: 15, of which 12 were waited for; matrix products, arithmetic and copies ran while one was open for 2% of the time, Pallas kernels for 3%

profile of v5, /device:TPU:1, one launch (start us, length us, event | category | flops | bytes accessed | tf_op | source)
XLA Modules:
  0.0 160.7 jit_solution(2328571329792427080)
XLA Ops:
  0.6 2.6 %pack.1 = bf16[8,64,1856]{2,1,0:T(8,128)(2,1)} custom-call(bf16[64,256]{1,0:T(8,128)(2,1)} %bitcast.24, bf16[64,256]{1,0:T(8,128)(2,1)} %bitcast.25, bf16[64,3584]{1,0:T(8,128)(2,1)} %gate_hbm.1, bf16[64,3584]{1,0:T(8,128)(2,1)} %up_hbm.1, bf16[64,3584]{1,0:T(8,128)(2,1)} %bitcast.23), custom_call_target="tpu_custom_call" | custom-call | tf_op jit(solution)/shard_map/pack/pallas_call | solution.py:91
  3.3 7.5 %all-to-all-start = ((bf16[8,64,1856]{2,1,0:T(8,128)(2,1)}), bf16[8,64,1856]{2,1,0:T(8,128)(2,1)S(1)}, u32[]{:S(2)}, u32[]{:S(2)}) async-start(bf16[8,64,1856]{2,1,0:T(8,128)(2,1)} %pack.1), calls=%async_computation | async-start | bytes 3932160 | tf_op jit(solution)/shard_map/all_to_all | solution.py:32
  10.7 1.7 %collective-permute-start.1 = (bf16[64,64]{1,0:T(8,128)(2,1)S(1)}, bf16[64,64]{1,0:T(8,128)(2,1)S(1)}, u32[]{:S(2)}, u32[]{:S(2)}) collective-permute-start(bf16[64,64]{1,0:T(8,128)(2,1)S(1)} %copy-done.2), channel_id=1, source_target_pairs={{0,1},{1,0},{2,3},{3,2},{4,5},{5,4},{6,7},{7,6},{8,9},{9,8},{10,11... | collective-permute-start | bytes 24584 | tf_op jit(solution)/shard_map/ppermute | solution.py:251
  12.5 1.1 collective-permute-done.1
  13.7 3.0 %collective-permute-start.2 = (bf16[64,128]{1,0:T(8,128)(2,1)S(1)}, bf16[64,128]{1,0:T(8,128)(2,1)S(1)}, u32[]{:S(2)}, u32[]{:S(2)}) collective-permute-start(bf16[64,128]{1,0:T(8,128)(2,1)S(1)} %pad_maximum_fusion.8), channel_id=1, source_target_pairs={{0,2},{1,3},{2,0},{3,1},{4,6},{5,7},{6,4},{7,5},{8,10},{9,11},{10,... | collective-permute-start | bytes 49160 | tf_op jit(solution)/shard_map/ppermute | solution.py:251
  16.7 1.4 collective-permute-done.2
  18.2 17.3 %all-to-all-done = bf16[8,64,1856]{2,1,0:T(8,128)(2,1)S(1)} async-done(((bf16[8,64,1856]{2,1,0:T(8,128)(2,1)}), bf16[8,64,1856]{2,1,0:T(8,128)(2,1)S(1)}, u32[]{:S(2)}, u32[]{:S(2)}) %all-to-all-start) | async-done | bytes 1900576 | tf_op jit(solution)/shard_map/all_to_all | solution.py:32
  35.5 0.3 convolution_convert_fusion.1
  35.9 0.5 convolution_convert_fusion
  36.3 0.1 copy.16
  36.5 0.9 pad_maximum_fusion.1
  37.4 8.2 %all-to-all-start.1 = ((bf16[8,32,1344]{2,1,0:T(8,128)(2,1)}), bf16[8,32,1344]{2,1,0:T(8,128)(2,1)S(1)}, u32[]{:S(2)}, u32[]{:S(2)}) async-start(bf16[8,32,1344]{2,1,0:T(8,128)(2,1)} %pad_maximum_fusion.1), calls=%async_computation.1 | async-start | bytes 1441792 | tf_op jit(solution)/shard_map/all_to_all | solution.py:32
  45.6 5.5 %collective-permute-start.3 = (bf16[64,256]{1,0:T(8,128)(2,1)S(1)}, bf16[64,256]{1,0:T(8,128)(2,1)S(1)}, u32[]{:S(2)}, u32[]{:S(2)}) collective-permute-start(bf16[64,256]{1,0:T(8,128)(2,1)S(1)} %pad_maximum_fusion.7), channel_id=1, source_target_pairs={{0,4},{1,5},{2,6},{3,7},{4,0},{5,1},{6,2},{7,3},{8,12},{9,13},{10,... | collective-permute-start | bytes 98312 | tf_op jit(solution)/shard_map/ppermute | solution.py:251
  51.1 18.1 %collective-permute-done.3 = bf16[64,256]{1,0:T(8,128)(2,1)S(1)} collective-permute-done((bf16[64,256]{1,0:T(8,128)(2,1)S(1)}, bf16[64,256]{1,0:T(8,128)(2,1)S(1)}, u32[]{:S(2)}, u32[]{:S(2)}) %collective-permute-start.3) | collective-permute-done | bytes 32800 | tf_op jit(solution)/shard_map/ppermute | solution.py:251
  69.2 0.1 collective-permute-start.4
  69.3 3.1 %collective-permute-done.4 = bf16[64,512]{1,0:T(8,128)(2,1)S(1)} collective-permute-done((bf16[64,512]{1,0:T(8,128)(2,1)S(1)}, bf16[64,512]{1,0:T(8,128)(2,1)S(1)}, u32[]{:S(2)}, u32[]{:S(2)}) %collective-permute-start.4) | collective-permute-done | bytes 65568 | tf_op jit(solution)/shard_map/ppermute | solution.py:251
  72.5 0.1 collective-permute-start.5
  72.6 5.3 %collective-permute-done.5 = bf16[64,1024]{1,0:T(8,128)(2,1)S(1)} collective-permute-done((bf16[64,1024]{1,0:T(8,128)(2,1)S(1)}, bf16[64,1024]{1,0:T(8,128)(2,1)S(1)}, u32[]{:S(2)}, u32[]{:S(2)}) %collective-permute-start.5) | collective-permute-done | bytes 131104 | tf_op jit(solution)/shard_map/ppermute | solution.py:251
  77.9 0.1 convert_reduce_fusion
  78.0 0.1 fusion.5
  78.2 0.8 broadcast_in_dim.4
  79.0 3.5 %all-to-all-start.2 = ((bf16[8,32,896]{2,1,0:T(8,128)(2,1)}), bf16[8,32,896]{2,1,0:T(8,128)(2,1)S(1)}, u32[]{:S(2)}, u32[]{:S(2)}) async-start(bf16[8,32,896]{2,1,0:T(8,128)(2,1)} %broadcast_in_dim.4), calls=%async_computation.2 | async-start | bytes 917504 | tf_op jit(solution)/shard_map/all_to_all | solution.py:32
  82.5 2.8 %collective-permute-start.6 = (bf16[64,2048]{1,0:T(8,128)(2,1)S(1)}, bf16[64,2048]{1,0:T(8,128)(2,1)S(1)}, u32[]{:S(2)}, u32[]{:S(2)}) collective-permute-start(bf16[64,2048]{1,0:T(8,128)(2,1)S(1)} %pad_maximum_fusion.3), channel_id=1, source_target_pairs={{0,32},{32,0},{1,33},{33,1},{2,34},{34,2},{3,35},{35,3},{4,36},{36... | collective-permute-start | bytes 786440 | tf_op jit(solution)/shard_map/ppermute | solution.py:251
  85.3 4.0 %collective-permute-done.6 = bf16[64,2048]{1,0:T(8,128)(2,1)S(1)} collective-permute-done((bf16[64,2048]{1,0:T(8,128)(2,1)S(1)}, bf16[64,2048]{1,0:T(8,128)(2,1)S(1)}, u32[]{:S(2)}, u32[]{:S(2)}) %collective-permute-start.6) | collective-permute-done | bytes 262176 | tf_op jit(solution)/shard_map/ppermute | solution.py:251
  89.3 0.1 broadcast_select_fusion.3
  89.4 6.0 %all-to-all-done.2 = bf16[8,32,896]{2,1,0:T(8,128)(2,1)S(1)} async-done(((bf16[8,32,896]{2,1,0:T(8,128)(2,1)}), bf16[8,32,896]{2,1,0:T(8,128)(2,1)S(1)}, u32[]{:S(2)}, u32[]{:S(2)}) %all-to-all-start.2) | async-done | bytes 458784 | tf_op jit(solution)/shard_map/all_to_all | solution.py:32
  95.4 1.2 backward.1
  96.6 9.7 %all-to-all-start.3 = ((bf16[32,8,512]{2,1,0:T(8,128)(2,1)}), bf16[32,8,512]{2,1,0:T(8,128)(2,1)S(1)}, u32[]{:S(2)}, u32[]{:S(2)}) async-start(bf16[32,8,512]{2,1,0:T(8,128)(2,1)} %bitcast.8), calls=%async_computation.3 | async-start | bytes 524288 | tf_op jit(solution)/shard_map/all_to_all | solution.py:32
  106.3 1.5 collective-permute-start.7
  107.8 0.1 dynamic-slice_bitcast_fusion
  108.0 6.7 %all-to-all-done.3 = bf16[32,8,512]{2,1,0:T(8,128)(2,1)S(1)} async-done(((bf16[32,8,512]{2,1,0:T(8,128)(2,1)}), bf16[32,8,512]{2,1,0:T(8,128)(2,1)S(1)}, u32[]{:S(2)}, u32[]{:S(2)}) %all-to-all-start.3) | async-done | bytes 262176 | tf_op jit(solution)/shard_map/all_to_all | solution.py:32
  114.8 0.6 broadcast_in_dim.5
  115.4 3.3 %all-to-all-start.4 = ((bf16[8,8,512]{2,1,0:T(8,128)(2,1)}), bf16[8,8,512]{2,1,0:T(8,128)(2,1)S(1)}, u32[]{:S(2)}, u32[]{:S(2)}) async-start(bf16[8,8,512]{2,1,0:T(8,128)(2,1)} %broadcast_in_dim.5), calls=%async_computation.4 | async-start | bytes 131072 | tf_op jit(solution)/shard_map/all_to_all | solution.py:32
  118.8 3.8 %collective-permute-done.7 = bf16[64,4096]{1,0:T(8,128)(2,1)} collective-permute-done((bf16[64,4096]{1,0:T(8,128)(2,1)S(1)}, bf16[64,4096]{1,0:T(8,128)(2,1)}, u32[]{:S(2)}, u32[]{:S(2)}) %collective-permute-start.7) | collective-permute-done | bytes 524320 | tf_op jit(solution)/shard_map/ppermute | solution.py:251
  122.6 2.0 %broadcast_select_fusion.1 = (bf16[64,4096]{1,0:T(8,128)(2,1)S(1)}, bf16[64,4096]{1,0:T(8,128)(2,1)}) fusion(bf16[64,4096]{1,0:T(8,128)(2,1)} %collective-permute-done.7, pred[]{:T(512)S(6)} %ne.21, bf16[64,2048]{1,0:T(8,128)(2,1)S(1)} %get-tuple-element.5, bf16[64,2048]{1,0:T(8,128)(2,1)S(1)} %get-tuple-element.4), kind=kLoop, calls=%fused_computation.10 | loop fusion | flops 1572864 | bytes 2097153 | tf_op jit(solution)/shard_map/jit(_where)/select_n | solution.py:254
  124.7 1.3 all-to-all-done.4.got_ref
  125.9 1.2 fan_out.1
  127.2 5.0 %all-to-all-start.5 = ((bf16[16,8,4096]{2,1,0:T(8,128)(2,1)}), bf16[16,8,4096]{2,1,0:T(8,128)(2,1)S(1)}, u32[]{:S(2)}, u32[]{:S(2)}) async-start(bf16[16,8,4096]{2,1,0:T(8,128)(2,1)} %fan_out.1), calls=%async_computation.5 | async-start | bytes 2097152 | tf_op jit(solution)/shard_map/all_to_all | solution.py:32
  132.2 0.1 pad_maximum_fusion.val_ref
  132.3 1.5 collective-permute-start.8
  133.8 12.7 %all-to-all-done.5 = bf16[16,8,4096]{2,1,0:T(8,128)(2,1)S(1)} async-done(((bf16[16,8,4096]{2,1,0:T(8,128)(2,1)}), bf16[16,8,4096]{2,1,0:T(8,128)(2,1)S(1)}, u32[]{:S(2)}, u32[]{:S(2)}) %all-to-all-start.5) | async-done | bytes 1048608 | tf_op jit(solution)/shard_map/all_to_all | solution.py:32
  146.5 3.4 %collective-permute-start = (bf16[128,4096]{1,0:T(8,128)(2,1)S(1)}, bf16[128,4096]{1,0:T(8,128)(2,1)S(1)}, u32[]{:S(2)}, u32[]{:S(2)}) collective-permute-start(bf16[128,4096]{1,0:T(8,128)(2,1)S(1)} %bitcast.17), channel_id=1, source_target_pairs={{0,64},{64,0},{1,65},{65,1},{2,66},{66,2},{3,67},{67,3},{4,68},{68... | collective-permute-start | bytes 3145736 | tf_op jit(solution)/shard_map/ppermute | solution.py:280
  149.9 2.5 %copy-done = bf16[640,4096]{1,0:T(8,128)(2,1)S(1)} copy-done((bf16[640,4096]{1,0:T(8,128)(2,1)S(1)}, bf16[640,4096]{1,0:T(8,128)(2,1)}, u32[]{:S(2)}) %copy-start) | copy-done | bytes 5242904
  152.4 2.3 %gram.2.gram_own_ref = f32[128,640]{1,0:T(8,128)S(1)} custom-call(bf16[640,4096]{1,0:T(8,128)(2,1)S(1)} %copy-done, bf16[128,4096]{1,0:T(8,128)(2,1)S(1)} %pad_maximum_fusion.val_ref), custom_call_target="tpu_custom_call" | custom-call | tf_op jit(solution)/shard_map/gram/pallas_call | solution.py:161
  154.7 2.3 %gram.3.gram_other_ref = f32[128,640]{1,0:T(8,128)S(1)} custom-call(bf16[640,4096]{1,0:T(8,128)(2,1)S(1)} %copy-done, bf16[128,4096]{1,0:T(8,128)(2,1)S(1)} %collective-permute-done.8.val_ref), custom_call_target="tpu_custom_call" | custom-call | tf_op jit(solution)/shard_map/gram/pallas_call | solution.py:161
  157.0 0.7 own_block.1
  157.7 0.5 slice-done.1
  158.3 2.4 %pair_values.1 = f32[640]{0:T(1024)} custom-call(bf16[640,4096]{1,0:T(8,128)(2,1)S(1)} %bitcast.16, bf16[128,4096]{1,0:T(8,128)(2,1)S(1)} %bitcast.19, bf16[128,4096]{1,0:T(8,128)(2,1)S(1)} %collective-permute-done.other_ref, f32[128,640]{1,0:T(8,128)S(1)} %gram.2.gram_own_ref, f32[128,640]{1,0:T(8,128)S(1)} %gram.3.gram_other_ref), custom_call_target="tpu_custom_call" | custom-call | tf_op jit(solution)/shard_map/pair_values/pallas_call | solution.py:211
  (28 shorter events, 0.6 us)
Async XLA Ops:
  3.2 7.5 %copy-start.2 = (bf16[64,64]{1,0:T(8,128)(2,1)S(1)}, bf16[64,64]{1,0:T(8,128)(2,1)}, u32[]{:S(2)}) copy-start(bf16[64,64]{1,0:T(8,128)(2,1)} %param.13) | copy-start | bytes 24580
  3.3 32.3 %all-to-all-start = ((bf16[8,64,1856]{2,1,0:T(8,128)(2,1)}), bf16[8,64,1856]{2,1,0:T(8,128)(2,1)S(1)}, u32[]{:S(2)}, u32[]{:S(2)}) async-start(bf16[8,64,1856]{2,1,0:T(8,128)(2,1)} %pack.1), calls=%async_computation | async-start | bytes 3932160 | tf_op jit(solution)/shard_map/all_to_all | solution.py:32
  10.7 2.9 %collective-permute-start.1 = (bf16[64,64]{1,0:T(8,128)(2,1)S(1)}, bf16[64,64]{1,0:T(8,128)(2,1)S(1)}, u32[]{:S(2)}, u32[]{:S(2)}) collective-permute-start(bf16[64,64]{1,0:T(8,128)(2,1)S(1)} %copy-done.2), channel_id=1, source_target_pairs={{0,1},{1,0},{2,3},{3,2},{4,5},{5,4},{6,7},{7,6},{8,9},{9,8},{10,11... | collective-permute-start | bytes 24584 | tf_op jit(solution)/shard_map/ppermute | solution.py:251
  13.7 4.4 %collective-permute-start.2 = (bf16[64,128]{1,0:T(8,128)(2,1)S(1)}, bf16[64,128]{1,0:T(8,128)(2,1)S(1)}, u32[]{:S(2)}, u32[]{:S(2)}) collective-permute-start(bf16[64,128]{1,0:T(8,128)(2,1)S(1)} %pad_maximum_fusion.8), channel_id=1, source_target_pairs={{0,2},{1,3},{2,0},{3,1},{4,6},{5,7},{6,4},{7,5},{8,10},{9,11},{10,... | collective-permute-start | bytes 49160 | tf_op jit(solution)/shard_map/ppermute | solution.py:251
  37.4 40.5 %all-to-all-start.1 = ((bf16[8,32,1344]{2,1,0:T(8,128)(2,1)}), bf16[8,32,1344]{2,1,0:T(8,128)(2,1)S(1)}, u32[]{:S(2)}, u32[]{:S(2)}) async-start(bf16[8,32,1344]{2,1,0:T(8,128)(2,1)} %pad_maximum_fusion.1), calls=%async_computation.1 | async-start | bytes 1441792 | tf_op jit(solution)/shard_map/all_to_all | solution.py:32
  45.6 23.6 %collective-permute-start.3 = (bf16[64,256]{1,0:T(8,128)(2,1)S(1)}, bf16[64,256]{1,0:T(8,128)(2,1)S(1)}, u32[]{:S(2)}, u32[]{:S(2)}) collective-permute-start(bf16[64,256]{1,0:T(8,128)(2,1)S(1)} %pad_maximum_fusion.7), channel_id=1, source_target_pairs={{0,4},{1,5},{2,6},{3,7},{4,0},{5,1},{6,2},{7,3},{8,12},{9,13},{10,... | collective-permute-start | bytes 98312 | tf_op jit(solution)/shard_map/ppermute | solution.py:251
  69.2 3.2 %collective-permute-start.4 = (bf16[64,512]{1,0:T(8,128)(2,1)S(1)}, bf16[64,512]{1,0:T(8,128)(2,1)S(1)}, u32[]{:S(2)}, u32[]{:S(2)}) collective-permute-start(bf16[64,512]{1,0:T(8,128)(2,1)S(1)} %pad_maximum_fusion.5), channel_id=1, source_target_pairs={{0,8},{8,0},{16,24},{24,16},{1,9},{9,1},{17,25},{25,17},{2,10},{10... | collective-permute-start | bytes 196616 | tf_op jit(solution)/shard_map/ppermute | solution.py:251
  72.5 5.4 %collective-permute-start.5 = (bf16[64,1024]{1,0:T(8,128)(2,1)S(1)}, bf16[64,1024]{1,0:T(8,128)(2,1)S(1)}, u32[]{:S(2)}, u32[]{:S(2)}) collective-permute-start(bf16[64,1024]{1,0:T(8,128)(2,1)S(1)} %pad_maximum_fusion.4), channel_id=1, source_target_pairs={{0,16},{8,24},{16,0},{24,8},{1,17},{9,25},{17,1},{25,9},{2,18},{10... | collective-permute-start | bytes 393224 | tf_op jit(solution)/shard_map/ppermute | solution.py:251
  79.0 16.4 %all-to-all-start.2 = ((bf16[8,32,896]{2,1,0:T(8,128)(2,1)}), bf16[8,32,896]{2,1,0:T(8,128)(2,1)S(1)}, u32[]{:S(2)}, u32[]{:S(2)}) async-start(bf16[8,32,896]{2,1,0:T(8,128)(2,1)} %broadcast_in_dim.4), calls=%async_computation.2 | async-start | bytes 917504 | tf_op jit(solution)/shard_map/all_to_all | solution.py:32
  82.5 6.8 %collective-permute-start.6 = (bf16[64,2048]{1,0:T(8,128)(2,1)S(1)}, bf16[64,2048]{1,0:T(8,128)(2,1)S(1)}, u32[]{:S(2)}, u32[]{:S(2)}) collective-permute-start(bf16[64,2048]{1,0:T(8,128)(2,1)S(1)} %pad_maximum_fusion.3), channel_id=1, source_target_pairs={{0,32},{32,0},{1,33},{33,1},{2,34},{34,2},{3,35},{35,3},{4,36},{36... | collective-permute-start | bytes 786440 | tf_op jit(solution)/shard_map/ppermute | solution.py:251
  96.6 18.1 %all-to-all-start.3 = ((bf16[32,8,512]{2,1,0:T(8,128)(2,1)}), bf16[32,8,512]{2,1,0:T(8,128)(2,1)S(1)}, u32[]{:S(2)}, u32[]{:S(2)}) async-start(bf16[32,8,512]{2,1,0:T(8,128)(2,1)} %bitcast.8), calls=%async_computation.3 | async-start | bytes 524288 | tf_op jit(solution)/shard_map/all_to_all | solution.py:32
  106.3 16.3 %collective-permute-start.7 = (bf16[64,4096]{1,0:T(8,128)(2,1)S(1)}, bf16[64,4096]{1,0:T(8,128)(2,1)}, u32[]{:S(2)}, u32[]{:S(2)}) collective-permute-start(bf16[64,4096]{1,0:T(8,128)(2,1)S(1)} %pad_maximum_fusion.2), channel_id=1, source_target_pairs={{0,128},{128,0},{1,129},{129,1},{2,130},{130,2},{3,131},{131,3},{4... | collective-permute-start | bytes 1572872 | tf_op jit(solution)/shard_map/ppermute | solution.py:251
  115.4 10.5 %all-to-all-start.4 = ((bf16[8,8,512]{2,1,0:T(8,128)(2,1)}), bf16[8,8,512]{2,1,0:T(8,128)(2,1)S(1)}, u32[]{:S(2)}, u32[]{:S(2)}) async-start(bf16[8,8,512]{2,1,0:T(8,128)(2,1)} %broadcast_in_dim.5), calls=%async_computation.4 | async-start | bytes 131072 | tf_op jit(solution)/shard_map/all_to_all | solution.py:32
  124.7 7.5 %copy-start.1 = (bf16[64,4096]{1,0:T(8,128)(2,1)S(1)}, bf16[64,4096]{1,0:T(8,128)(2,1)}, u32[]{:S(2)}) copy-start(bf16[64,4096]{1,0:T(8,128)(2,1)} %get-tuple-element.3) | copy-start | bytes 1572868
  127.2 19.3 %all-to-all-start.5 = ((bf16[16,8,4096]{2,1,0:T(8,128)(2,1)}), bf16[16,8,4096]{2,1,0:T(8,128)(2,1)S(1)}, u32[]{:S(2)}, u32[]{:S(2)}) async-start(bf16[16,8,4096]{2,1,0:T(8,128)(2,1)} %fan_out.1), calls=%async_computation.5 | async-start | bytes 2097152 | tf_op jit(solution)/shard_map/all_to_all | solution.py:32
  132.3 22.4 %collective-permute-start.8 = (bf16[128,4096]{1,0:T(8,128)(2,1)S(1)}, bf16[128,4096]{1,0:T(8,128)(2,1)S(1)}, u32[]{:S(2)}, u32[]{:S(2)}) collective-permute-start(bf16[128,4096]{1,0:T(8,128)(2,1)S(1)} %pad_maximum_fusion.val_ref), channel_id=1, source_target_pairs={{0,64},{64,0},{1,65},{65,1},{2,66},{66,2},{3,67},{67,3},{4,68},{68... | collective-permute-start | bytes 3145736 | tf_op jit(solution)/shard_map/ppermute | solution.py:267
  146.5 11.3 %collective-permute-start = (bf16[128,4096]{1,0:T(8,128)(2,1)S(1)}, bf16[128,4096]{1,0:T(8,128)(2,1)S(1)}, u32[]{:S(2)}, u32[]{:S(2)}) collective-permute-start(bf16[128,4096]{1,0:T(8,128)(2,1)S(1)} %bitcast.17), channel_id=1, source_target_pairs={{0,64},{64,0},{1,65},{65,1},{2,66},{66,2},{3,67},{67,3},{4,68},{68... | collective-permute-start | bytes 3145736 | tf_op jit(solution)/shard_map/ppermute | solution.py:280
  149.9 2.5 %copy-start = (bf16[640,4096]{1,0:T(8,128)(2,1)S(1)}, bf16[640,4096]{1,0:T(8,128)(2,1)}, u32[]{:S(2)}) copy-start(bf16[640,4096]{1,0:T(8,128)(2,1)} %train_ref.4) | copy-start | bytes 15728644
  154.7 3.1 %slice-start = ((s8[5242880]{0:T(1024)(128)(4,1)}), s8[4194304]{0:T(1024)(128)(4,1)S(1)}, s32[]{:S(2)}) async-start(s8[5242880]{0:T(1024)(128)(4,1)} %bitcast.15), calls=%async_computation.6 | async-start | bytes 8388608
  157.0 1.2 slice-start.1

commit v6 on v5

--- a/solution.py
+++ b/solution.py
@@ -225,6 +225,33 @@
     return jnp.concatenate([grad_gate, grad_up], axis=1)
 
 
+def act_kernel(parts_ref, out_ref, held, sems):
+    pre = jnp.sum(parts_ref[...].astype(F32), axis=0)
+    own = pre.shape[1] // 3
+    held[...] = act_grads(pre[:, :own], pre[:, own : 2 * own], pre[:, 2 * own :])
+    copies = [
+        pltpu.make_async_copy(held, out_ref.at[i], sems.at[i]) for i in range(out_ref.shape[0])
+    ]
+    for copy in copies:
+        copy.start()
+    for copy in copies:
+        copy.wait()
+
+
+def act_slots(parts):
+    count, rows, wide = parts.shape
+    kept = 2 * wide // 3
+    return pl.pallas_call(
+        act_kernel,
+        in_specs=[pl.BlockSpec(memory_space=pltpu.VMEM)],
+        out_specs=pl.BlockSpec(memory_space=pl.ANY),
+        out_shape=jax.ShapeDtypeStruct((count, rows, kept), BF16),
+        scratch_shapes=[pltpu.VMEM((rows, kept), BF16), pltpu.SemaphoreType.DMA((count,))],
+        compiler_params=pltpu.CompilerParams(vmem_limit_bytes=4 * 1024 * 1024),
+        name="act_slots",
+    )(parts)
+
+
 def local(
     val_inputs, val_out_grad, w_gate, w_up, w_down, val_attn_inputs, train_inputs, train_grads
 ):
@@ -261,9 +288,8 @@
         axis=1,
     ).astype(BF16)
     parts = trade(partial.reshape(n_z, rows_z, 3 * own), "z")
-    pre = jnp.sum(parts.astype(F32), axis=0)
-    grads = act_grads(pre[:, :own], pre[:, own : 2 * own], pre[:, 2 * own :])
-    grads = share(grads, "z", n_z).reshape(vals, 2 * own)
+    sent = act_slots(parts)
+    grads = trade(sent, "z").reshape(vals, 2 * own)
     attn_other = lax.ppermute(attn, "c", swap)
     part = backward(first_w, grads, got)
     parts = trade(part.reshape(n_hidplane, chunk, wide), HIDPLANE)

time: 161 us -> 161 us (level)
  no operation moved by 1% of the time
where the time goes in v6:
time: 161 us
  waiting for transfers between devices  80.9 us (50%)
  starting transfers between devices  56.7 us (35%)
  Pallas kernels  13.8 us (9%)
  local copies, waits for them, and re-layouts  3.99 us (2%)
  other arithmetic  3.56 us (2%)
    all_to_all x6, waiting for transfers between devices, trade(): return lax.all_to_all(value, axes, 0, 0, tiled=True)  43.9 us
    all_to_all x6, starting transfers between devices, trade(): return lax.all_to_all(value, axes, 0, 0, tiled=True)  37.2 us
    ppermute x7, waiting for transfers between devices, local(): theirs = lax.ppermute(attn, axis, pairs)  36.9 us
    ppermute x7, starting transfers between devices, local(): theirs = lax.ppermute(attn, axis, pairs)  14.6 us
    pallas_call x2, Pallas kernels, gram(): pl.pallas_call(gram_kernel, grid=(tokens // block,), in_specs=[pl.BlockSp...  4.62 us
    ppermute x1, starting transfers between devices, local(): val_other = lax.ppermute(val_own, 'c', swap)  3.46 us
  transfers between devices with their start and end apart: 15, of which 12 were waited for; matrix products, arithmetic and copies ran while one was open for 2% of the time, Pallas kernels for 3%

profile of v6, /device:TPU:1, one launch (start us, length us, event | category | flops | bytes accessed | tf_op | source)
XLA Modules:
  0.0 160.7 jit_solution(11085065551365801795)
XLA Ops:
  0.6 2.6 %pack.1 = bf16[8,64,1856]{2,1,0:T(8,128)(2,1)} custom-call(bf16[64,256]{1,0:T(8,128)(2,1)} %bitcast.24, bf16[64,256]{1,0:T(8,128)(2,1)} %bitcast.25, bf16[64,3584]{1,0:T(8,128)(2,1)} %gate_hbm.1, bf16[64,3584]{1,0:T(8,128)(2,1)} %up_hbm.1, bf16[64,3584]{1,0:T(8,128)(2,1)} %bitcast.23), custom_call_target="tpu_custom_call" | custom-call | tf_op jit(solution)/shard_map/pack/pallas_call | solution.py:91
  3.3 7.5 %all-to-all-start = ((bf16[8,64,1856]{2,1,0:T(8,128)(2,1)}), bf16[8,64,1856]{2,1,0:T(8,128)(2,1)S(1)}, u32[]{:S(2)}, u32[]{:S(2)}) async-start(bf16[8,64,1856]{2,1,0:T(8,128)(2,1)} %pack.1), calls=%async_computation | async-start | bytes 3932160 | tf_op jit(solution)/shard_map/all_to_all | solution.py:32
  10.8 1.7 %collective-permute-start.1 = (bf16[64,64]{1,0:T(8,128)(2,1)S(1)}, bf16[64,64]{1,0:T(8,128)(2,1)S(1)}, u32[]{:S(2)}, u32[]{:S(2)}) collective-permute-start(bf16[64,64]{1,0:T(8,128)(2,1)S(1)} %copy-done.2), channel_id=1, source_target_pairs={{0,1},{1,0},{2,3},{3,2},{4,5},{5,4},{6,7},{7,6},{8,9},{9,8},{10,11... | collective-permute-start | bytes 24584 | tf_op jit(solution)/shard_map/ppermute | solution.py:278
  12.5 1.1 collective-permute-done.1
  13.6 0.1 pad_maximum_fusion.7
  13.7 3.0 %collective-permute-start.2 = (bf16[64,128]{1,0:T(8,128)(2,1)S(1)}, bf16[64,128]{1,0:T(8,128)(2,1)S(1)}, u32[]{:S(2)}, u32[]{:S(2)}) collective-permute-start(bf16[64,128]{1,0:T(8,128)(2,1)S(1)} %pad_maximum_fusion.7), channel_id=1, source_target_pairs={{0,2},{1,3},{2,0},{3,1},{4,6},{5,7},{6,4},{7,5},{8,10},{9,11},{10,... | collective-permute-start | bytes 49160 | tf_op jit(solution)/shard_map/ppermute | solution.py:278
  16.7 1.4 collective-permute-done.2
  18.2 0.1 broadcast_select_fusion.13
  18.2 17.3 %all-to-all-done = bf16[8,64,1856]{2,1,0:T(8,128)(2,1)S(1)} async-done(((bf16[8,64,1856]{2,1,0:T(8,128)(2,1)}), bf16[8,64,1856]{2,1,0:T(8,128)(2,1)S(1)}, u32[]{:S(2)}, u32[]{:S(2)}) %all-to-all-start) | async-done | bytes 1900576 | tf_op jit(solution)/shard_map/all_to_all | solution.py:32
  35.6 0.3 convolution_convert_fusion.1
  35.9 0.5 convolution_convert_fusion
  36.4 0.1 copy.14
  36.5 0.9 pad_maximum_fusion.1
  37.5 8.2 %all-to-all-start.1 = ((bf16[8,32,1344]{2,1,0:T(8,128)(2,1)}), bf16[8,32,1344]{2,1,0:T(8,128)(2,1)S(1)}, u32[]{:S(2)}, u32[]{:S(2)}) async-start(bf16[8,32,1344]{2,1,0:T(8,128)(2,1)} %pad_maximum_fusion.1), calls=%async_computation.1 | async-start | bytes 1441792 | tf_op jit(solution)/shard_map/all_to_all | solution.py:32
  45.6 5.5 %collective-permute-start.3 = (bf16[64,256]{1,0:T(8,128)(2,1)S(1)}, bf16[64,256]{1,0:T(8,128)(2,1)S(1)}, u32[]{:S(2)}, u32[]{:S(2)}) collective-permute-start(bf16[64,256]{1,0:T(8,128)(2,1)S(1)} %pad_maximum_fusion.6), channel_id=1, source_target_pairs={{0,4},{1,5},{2,6},{3,7},{4,0},{5,1},{6,2},{7,3},{8,12},{9,13},{10,... | collective-permute-start | bytes 98312 | tf_op jit(solution)/shard_map/ppermute | solution.py:278
  51.1 18.1 %collective-permute-done.3 = bf16[64,256]{1,0:T(8,128)(2,1)S(1)} collective-permute-done((bf16[64,256]{1,0:T(8,128)(2,1)S(1)}, bf16[64,256]{1,0:T(8,128)(2,1)S(1)}, u32[]{:S(2)}, u32[]{:S(2)}) %collective-permute-start.3) | collective-permute-done | bytes 32800 | tf_op jit(solution)/shard_map/ppermute | solution.py:278
  69.2 0.1 collective-permute-start.4
  69.4 3.1 %collective-permute-done.4 = bf16[64,512]{1,0:T(8,128)(2,1)S(1)} collective-permute-done((bf16[64,512]{1,0:T(8,128)(2,1)S(1)}, bf16[64,512]{1,0:T(8,128)(2,1)S(1)}, u32[]{:S(2)}, u32[]{:S(2)}) %collective-permute-start.4) | collective-permute-done | bytes 65568 | tf_op jit(solution)/shard_map/ppermute | solution.py:278
  72.5 0.1 collective-permute-start.5
  72.6 5.3 %collective-permute-done.5 = bf16[64,1024]{1,0:T(8,128)(2,1)S(1)} collective-permute-done((bf16[64,1024]{1,0:T(8,128)(2,1)S(1)}, bf16[64,1024]{1,0:T(8,128)(2,1)S(1)}, u32[]{:S(2)}, u32[]{:S(2)}) %collective-permute-start.5) | collective-permute-done | bytes 131104 | tf_op jit(solution)/shard_map/ppermute | solution.py:278
  78.0 1.0 act_slots.1
  79.0 3.5 %all-to-all-start.2 = ((bf16[8,32,896]{2,1,0:T(8,128)(2,1)}), bf16[8,32,896]{2,1,0:T(8,128)(2,1)S(1)}, u32[]{:S(2)}, u32[]{:S(2)}) async-start(bf16[8,32,896]{2,1,0:T(8,128)(2,1)} %act_slots.1), calls=%async_computation.2 | async-start | bytes 917504 | tf_op jit(solution)/shard_map/all_to_all | solution.py:32
  82.5 2.8 %collective-permute-start.6 = (bf16[64,2048]{1,0:T(8,128)(2,1)S(1)}, bf16[64,2048]{1,0:T(8,128)(2,1)S(1)}, u32[]{:S(2)}, u32[]{:S(2)}) collective-permute-start(bf16[64,2048]{1,0:T(8,128)(2,1)S(1)} %pad_maximum_fusion.3), channel_id=1, source_target_pairs={{0,32},{32,0},{1,33},{33,1},{2,34},{34,2},{3,35},{35,3},{4,36},{36... | collective-permute-start | bytes 786440 | tf_op jit(solution)/shard_map/ppermute | solution.py:278
  85.3 4.0 %collective-permute-done.6 = bf16[64,2048]{1,0:T(8,128)(2,1)S(1)} collective-permute-done((bf16[64,2048]{1,0:T(8,128)(2,1)S(1)}, bf16[64,2048]{1,0:T(8,128)(2,1)S(1)}, u32[]{:S(2)}, u32[]{:S(2)}) %collective-permute-start.6) | collective-permute-done | bytes 262176 | tf_op jit(solution)/shard_map/ppermute | solution.py:278
  89.3 0.1 broadcast_select_fusion.3
  89.4 6.0 %all-to-all-done.2 = bf16[8,32,896]{2,1,0:T(8,128)(2,1)S(1)} async-done(((bf16[8,32,896]{2,1,0:T(8,128)(2,1)}), bf16[8,32,896]{2,1,0:T(8,128)(2,1)S(1)}, u32[]{:S(2)}, u32[]{:S(2)}) %all-to-all-start.2) | async-done | bytes 458784 | tf_op jit(solution)/shard_map/all_to_all | solution.py:32
  95.4 1.2 backward.1
  96.6 9.7 %all-to-all-start.3 = ((bf16[32,8,512]{2,1,0:T(8,128)(2,1)}), bf16[32,8,512]{2,1,0:T(8,128)(2,1)S(1)}, u32[]{:S(2)}, u32[]{:S(2)}) async-start(bf16[32,8,512]{2,1,0:T(8,128)(2,1)} %bitcast.8), calls=%async_computation.3 | async-start | bytes 524288 | tf_op jit(solution)/shard_map/all_to_all | solution.py:32
  106.3 1.5 collective-permute-start.7
  107.8 0.1 dynamic-slice_bitcast_fusion
  108.0 6.7 %all-to-all-done.3 = bf16[32,8,512]{2,1,0:T(8,128)(2,1)S(1)} async-done(((bf16[32,8,512]{2,1,0:T(8,128)(2,1)}), bf16[32,8,512]{2,1,0:T(8,128)(2,1)S(1)}, u32[]{:S(2)}, u32[]{:S(2)}) %all-to-all-start.3) | async-done | bytes 262176 | tf_op jit(solution)/shard_map/all_to_all | solution.py:32
  114.8 0.6 broadcast_in_dim.2
  115.4 3.3 %all-to-all-start.4 = ((bf16[8,8,512]{2,1,0:T(8,128)(2,1)}), bf16[8,8,512]{2,1,0:T(8,128)(2,1)S(1)}, u32[]{:S(2)}, u32[]{:S(2)}) async-start(bf16[8,8,512]{2,1,0:T(8,128)(2,1)} %broadcast_in_dim.2), calls=%async_computation.4 | async-start | bytes 131072 | tf_op jit(solution)/shard_map/all_to_all | solution.py:32
  118.8 3.8 %collective-permute-done.7 = bf16[64,4096]{1,0:T(8,128)(2,1)} collective-permute-done((bf16[64,4096]{1,0:T(8,128)(2,1)S(1)}, bf16[64,4096]{1,0:T(8,128)(2,1)}, u32[]{:S(2)}, u32[]{:S(2)}) %collective-permute-start.7) | collective-permute-done | bytes 524320 | tf_op jit(solution)/shard_map/ppermute | solution.py:278
  122.6 2.0 %broadcast_select_fusion.1 = (bf16[64,4096]{1,0:T(8,128)(2,1)S(1)}, bf16[64,4096]{1,0:T(8,128)(2,1)}) fusion(bf16[64,4096]{1,0:T(8,128)(2,1)} %collective-permute-done.7, pred[]{:T(512)S(6)} %ne.21, bf16[64,2048]{1,0:T(8,128)(2,1)S(1)} %get-tuple-element.5, bf16[64,2048]{1,0:T(8,128)(2,1)S(1)} %get-tuple-element.4), kind=kLoop, calls=%fused_computation.9 | loop fusion | flops 1572864 | bytes 2097153 | tf_op jit(solution)/shard_map/jit(_where)/select_n | solution.py:281
  124.7 1.3 all-to-all-done.4.got_ref
  125.9 1.2 fan_out.1
  127.2 5.0 %all-to-all-start.5 = ((bf16[16,8,4096]{2,1,0:T(8,128)(2,1)}), bf16[16,8,4096]{2,1,0:T(8,128)(2,1)S(1)}, u32[]{:S(2)}, u32[]{:S(2)}) async-start(bf16[16,8,4096]{2,1,0:T(8,128)(2,1)} %fan_out.1), calls=%async_computation.5 | async-start | bytes 2097152 | tf_op jit(solution)/shard_map/all_to_all | solution.py:32
  132.2 0.1 pad_maximum_fusion.val_ref
  132.3 1.5 collective-permute-start.8
  133.8 12.6 %all-to-all-done.5 = bf16[16,8,4096]{2,1,0:T(8,128)(2,1)S(1)} async-done(((bf16[16,8,4096]{2,1,0:T(8,128)(2,1)}), bf16[16,8,4096]{2,1,0:T(8,128)(2,1)S(1)}, u32[]{:S(2)}, u32[]{:S(2)}) %all-to-all-start.5) | async-done | bytes 1048608 | tf_op jit(solution)/shard_map/all_to_all | solution.py:32
  146.4 3.5 %collective-permute-start = (bf16[128,4096]{1,0:T(8,128)(2,1)S(1)}, bf16[128,4096]{1,0:T(8,128)(2,1)S(1)}, u32[]{:S(2)}, u32[]{:S(2)}) collective-permute-start(bf16[128,4096]{1,0:T(8,128)(2,1)S(1)} %bitcast.17), channel_id=1, source_target_pairs={{0,64},{64,0},{1,65},{65,1},{2,66},{66,2},{3,67},{67,3},{4,68},{68... | collective-permute-start | bytes 3145736 | tf_op jit(solution)/shard_map/ppermute | solution.py:306
  149.9 2.5 %copy-done = bf16[640,4096]{1,0:T(8,128)(2,1)S(1)} copy-done((bf16[640,4096]{1,0:T(8,128)(2,1)S(1)}, bf16[640,4096]{1,0:T(8,128)(2,1)}, u32[]{:S(2)}) %copy-start) | copy-done | bytes 5242904
  152.3 2.3 %gram.2.gram_own_ref = f32[128,640]{1,0:T(8,128)S(1)} custom-call(bf16[640,4096]{1,0:T(8,128)(2,1)S(1)} %copy-done, bf16[128,4096]{1,0:T(8,128)(2,1)S(1)} %pad_maximum_fusion.val_ref), custom_call_target="tpu_custom_call" | custom-call | tf_op jit(solution)/shard_map/gram/pallas_call | solution.py:161
  154.7 2.3 %gram.3.gram_other_ref = f32[128,640]{1,0:T(8,128)S(1)} custom-call(bf16[640,4096]{1,0:T(8,128)(2,1)S(1)} %copy-done, bf16[128,4096]{1,0:T(8,128)(2,1)S(1)} %collective-permute-done.8.val_ref), custom_call_target="tpu_custom_call" | custom-call | tf_op jit(solution)/shard_map/gram/pallas_call | solution.py:161
  157.0 0.7 own_block.1
  157.7 0.5 slice-done.1
  158.2 2.4 %pair_values.1 = f32[640]{0:T(1024)} custom-call(bf16[640,4096]{1,0:T(8,128)(2,1)S(1)} %bitcast.16, bf16[128,4096]{1,0:T(8,128)(2,1)S(1)} %bitcast.19, bf16[128,4096]{1,0:T(8,128)(2,1)S(1)} %collective-permute-done.other_ref, f32[128,640]{1,0:T(8,128)S(1)} %gram.2.gram_own_ref, f32[128,640]{1,0:T(8,128)S(1)} %gram.3.gram_other_ref), custom_call_target="tpu_custom_call" | custom-call | tf_op jit(solution)/shard_map/pair_values/pallas_call | solution.py:211
  (25 shorter events, 0.3 us)
Async XLA Ops:
  3.3 7.5 %copy-start.2 = (bf16[64,64]{1,0:T(8,128)(2,1)S(1)}, bf16[64,64]{1,0:T(8,128)(2,1)}, u32[]{:S(2)}) copy-start(bf16[64,64]{1,0:T(8,128)(2,1)} %param.13) | copy-start | bytes 24580
  3.3 32.3 %all-to-all-start = ((bf16[8,64,1856]{2,1,0:T(8,128)(2,1)}), bf16[8,64,1856]{2,1,0:T(8,128)(2,1)S(1)}, u32[]{:S(2)}, u32[]{:S(2)}) async-start(bf16[8,64,1856]{2,1,0:T(8,128)(2,1)} %pack.1), calls=%async_computation | async-start | bytes 3932160 | tf_op jit(solution)/shard_map/all_to_all | solution.py:32
  10.8 2.9 %collective-permute-start.1 = (bf16[64,64]{1,0:T(8,128)(2,1)S(1)}, bf16[64,64]{1,0:T(8,128)(2,1)S(1)}, u32[]{:S(2)}, u32[]{:S(2)}) collective-permute-start(bf16[64,64]{1,0:T(8,128)(2,1)S(1)} %copy-done.2), channel_id=1, source_target_pairs={{0,1},{1,0},{2,3},{3,2},{4,5},{5,4},{6,7},{7,6},{8,9},{9,8},{10,11... | collective-permute-start | bytes 24584 | tf_op jit(solution)/shard_map/ppermute | solution.py:278
  13.7 4.4 %collective-permute-start.2 = (bf16[64,128]{1,0:T(8,128)(2,1)S(1)}, bf16[64,128]{1,0:T(8,128)(2,1)S(1)}, u32[]{:S(2)}, u32[]{:S(2)}) collective-permute-start(bf16[64,128]{1,0:T(8,128)(2,1)S(1)} %pad_maximum_fusion.7), channel_id=1, source_target_pairs={{0,2},{1,3},{2,0},{3,1},{4,6},{5,7},{6,4},{7,5},{8,10},{9,11},{10,... | collective-permute-start | bytes 49160 | tf_op jit(solution)/shard_map/ppermute | solution.py:278
  37.5 40.5 %all-to-all-start.1 = ((bf16[8,32,1344]{2,1,0:T(8,128)(2,1)}), bf16[8,32,1344]{2,1,0:T(8,128)(2,1)S(1)}, u32[]{:S(2)}, u32[]{:S(2)}) async-start(bf16[8,32,1344]{2,1,0:T(8,128)(2,1)} %pad_maximum_fusion.1), calls=%async_computation.1 | async-start | bytes 1441792 | tf_op jit(solution)/shard_map/all_to_all | solution.py:32
  45.6 23.6 %collective-permute-start.3 = (bf16[64,256]{1,0:T(8,128)(2,1)S(1)}, bf16[64,256]{1,0:T(8,128)(2,1)S(1)}, u32[]{:S(2)}, u32[]{:S(2)}) collective-permute-start(bf16[64,256]{1,0:T(8,128)(2,1)S(1)} %pad_maximum_fusion.6), channel_id=1, source_target_pairs={{0,4},{1,5},{2,6},{3,7},{4,0},{5,1},{6,2},{7,3},{8,12},{9,13},{10,... | collective-permute-start | bytes 98312 | tf_op jit(solution)/shard_map/ppermute | solution.py:278
  69.2 3.2 %collective-permute-start.4 = (bf16[64,512]{1,0:T(8,128)(2,1)S(1)}, bf16[64,512]{1,0:T(8,128)(2,1)S(1)}, u32[]{:S(2)}, u32[]{:S(2)}) collective-permute-start(bf16[64,512]{1,0:T(8,128)(2,1)S(1)} %pad_maximum_fusion.5), channel_id=1, source_target_pairs={{0,8},{8,0},{16,24},{24,16},{1,9},{9,1},{17,25},{25,17},{2,10},{10... | collective-permute-start | bytes 196616 | tf_op jit(solution)/shard_map/ppermute | solution.py:278
  72.5 5.4 %collective-permute-start.5 = (bf16[64,1024]{1,0:T(8,128)(2,1)S(1)}, bf16[64,1024]{1,0:T(8,128)(2,1)S(1)}, u32[]{:S(2)}, u32[]{:S(2)}) collective-permute-start(bf16[64,1024]{1,0:T(8,128)(2,1)S(1)} %pad_maximum_fusion.4), channel_id=1, source_target_pairs={{0,16},{8,24},{16,0},{24,8},{1,17},{9,25},{17,1},{25,9},{2,18},{10... | collective-permute-start | bytes 393224 | tf_op jit(solution)/shard_map/ppermute | solution.py:278
  79.0 16.4 %all-to-all-start.2 = ((bf16[8,32,896]{2,1,0:T(8,128)(2,1)}), bf16[8,32,896]{2,1,0:T(8,128)(2,1)S(1)}, u32[]{:S(2)}, u32[]{:S(2)}) async-start(bf16[8,32,896]{2,1,0:T(8,128)(2,1)} %act_slots.1), calls=%async_computation.2 | async-start | bytes 917504 | tf_op jit(solution)/shard_map/all_to_all | solution.py:32
  82.5 6.8 %collective-permute-start.6 = (bf16[64,2048]{1,0:T(8,128)(2,1)S(1)}, bf16[64,2048]{1,0:T(8,128)(2,1)S(1)}, u32[]{:S(2)}, u32[]{:S(2)}) collective-permute-start(bf16[64,2048]{1,0:T(8,128)(2,1)S(1)} %pad_maximum_fusion.3), channel_id=1, source_target_pairs={{0,32},{32,0},{1,33},{33,1},{2,34},{34,2},{3,35},{35,3},{4,36},{36... | collective-permute-start | bytes 786440 | tf_op jit(solution)/shard_map/ppermute | solution.py:278
  96.6 18.1 %all-to-all-start.3 = ((bf16[32,8,512]{2,1,0:T(8,128)(2,1)}), bf16[32,8,512]{2,1,0:T(8,128)(2,1)S(1)}, u32[]{:S(2)}, u32[]{:S(2)}) async-start(bf16[32,8,512]{2,1,0:T(8,128)(2,1)} %bitcast.8), calls=%async_computation.3 | async-start | bytes 524288 | tf_op jit(solution)/shard_map/all_to_all | solution.py:32
  106.3 16.3 %collective-permute-start.7 = (bf16[64,4096]{1,0:T(8,128)(2,1)S(1)}, bf16[64,4096]{1,0:T(8,128)(2,1)}, u32[]{:S(2)}, u32[]{:S(2)}) collective-permute-start(bf16[64,4096]{1,0:T(8,128)(2,1)S(1)} %pad_maximum_fusion.2), channel_id=1, source_target_pairs={{0,128},{128,0},{1,129},{129,1},{2,130},{130,2},{3,131},{131,3},{4... | collective-permute-start | bytes 1572872 | tf_op jit(solution)/shard_map/ppermute | solution.py:278
  115.4 10.5 %all-to-all-start.4 = ((bf16[8,8,512]{2,1,0:T(8,128)(2,1)}), bf16[8,8,512]{2,1,0:T(8,128)(2,1)S(1)}, u32[]{:S(2)}, u32[]{:S(2)}) async-start(bf16[8,8,512]{2,1,0:T(8,128)(2,1)} %broadcast_in_dim.2), calls=%async_computation.4 | async-start | bytes 131072 | tf_op jit(solution)/shard_map/all_to_all | solution.py:32
  124.7 7.5 %copy-start.1 = (bf16[64,4096]{1,0:T(8,128)(2,1)S(1)}, bf16[64,4096]{1,0:T(8,128)(2,1)}, u32[]{:S(2)}) copy-start(bf16[64,4096]{1,0:T(8,128)(2,1)} %get-tuple-element.3) | copy-start | bytes 1572868
  127.2 19.2 %all-to-all-start.5 = ((bf16[16,8,4096]{2,1,0:T(8,128)(2,1)}), bf16[16,8,4096]{2,1,0:T(8,128)(2,1)S(1)}, u32[]{:S(2)}, u32[]{:S(2)}) async-start(bf16[16,8,4096]{2,1,0:T(8,128)(2,1)} %fan_out.1), calls=%async_computation.5 | async-start | bytes 2097152 | tf_op jit(solution)/shard_map/all_to_all | solution.py:32
  132.3 22.4 %collective-permute-start.8 = (bf16[128,4096]{1,0:T(8,128)(2,1)S(1)}, bf16[128,4096]{1,0:T(8,128)(2,1)S(1)}, u32[]{:S(2)}, u32[]{:S(2)}) collective-permute-start(bf16[128,4096]{1,0:T(8,128)(2,1)S(1)} %pad_maximum_fusion.val_ref), channel_id=1, source_target_pairs={{0,64},{64,0},{1,65},{65,1},{2,66},{66,2},{3,67},{67,3},{4,68},{68... | collective-permute-start | bytes 3145736 | tf_op jit(solution)/shard_map/ppermute | solution.py:293
  146.4 11.3 %collective-permute-start = (bf16[128,4096]{1,0:T(8,128)(2,1)S(1)}, bf16[128,4096]{1,0:T(8,128)(2,1)S(1)}, u32[]{:S(2)}, u32[]{:S(2)}) collective-permute-start(bf16[128,4096]{1,0:T(8,128)(2,1)S(1)} %bitcast.17), channel_id=1, source_target_pairs={{0,64},{64,0},{1,65},{65,1},{2,66},{66,2},{3,67},{67,3},{4,68},{68... | collective-permute-start | bytes 3145736 | tf_op jit(solution)/shard_map/ppermute | solution.py:306
  149.9 2.5 %copy-start = (bf16[640,4096]{1,0:T(8,128)(2,1)S(1)}, bf16[640,4096]{1,0:T(8,128)(2,1)}, u32[]{:S(2)}) copy-start(bf16[640,4096]{1,0:T(8,128)(2,1)} %train_ref.4) | copy-start | bytes 15728644
  154.7 3.1 %slice-start = ((s8[5242880]{0:T(1024)(128)(4,1)}), s8[4194304]{0:T(1024)(128)(4,1)S(1)}, s32[]{:S(2)}) async-start(s8[5242880]{0:T(1024)(128)(4,1)} %bitcast.15), calls=%async_computation.6 | async-start | bytes 8388608
  157.0 1.2 slice-start.1
